TPU v7x, 128 devices: a whole 4x4x4 slice. The times are simulated.
128 devices in a mesh: dp: 16 (over z, x), tm: 8 (over y, core).
Axes of the slice: x: 4, y: 4, z: 4, core: 2. Of those that a mesh axis runs over, the one named last changes fastest.
Arguments:
- frames: bfloat16 [16, 6144, 1024], P('dp', 'tm'), may hold values from -18 to 18
- lengths: int32 [16], P('dp'), may hold values from 1 to 6144, 58982 in all
- w_in: bfloat16 [1024, 2048], replicated, may hold values from -4 to 4
- w_dw: float32 [31, 1024], replicated, may hold values from -1 to 1
- bn_gain: float32 [1024], replicated, may hold values from 0.25 to 1.75
- bn_bias: float32 [1024], replicated, may hold values from -1 to 1
- w_out: bfloat16 [1024, 1024], replicated, may hold values from -0.1875 to 0.1875
- cotangent: bfloat16 [16, 6144, 1024], P('dp', 'tm'), may hold values from -6 to 6
Outputs:
- output: bfloat16 [16, 6144, 1024], P('dp', 'tm')
- grad_frames: bfloat16 [16, 6144, 1024], P('dp', 'tm')
- grad_w_in: float32 [1024, 2048], P(('dp', 'tm'))
- grad_w_out: float32 [1024, 1024], P(('dp', 'tm'))
- grad_kernel: float32 [31, 1024], replicated
- grad_gain: float32 [1024], replicated
- grad_bias: float32 [1024], replicated
Inputs may be any that keep to these rules, and one draw needn't show every extreme that they name: Frame slots at or after a recording's length are padding; the lengths sum to 58982 and the longest is exactly 6144.
All inputs are finite; a program needn't handle non-finite values. No bound on the sum of `lengths` on one device may be relied on, other than what follows from the above.
Results may differ from a plain program's by a relative error of at most 0.015.
Values may be sent and summed in bfloat16 or wider, within the bound.
A program may use at most 128 MiB of HBM per device.

v0:
```python
import math

import jax
import jax.numpy as jnp
from jax import lax
from jax.sharding import PartitionSpec as P


def padded_2(cells, sides, width):
    for axis, dim in sides:
        count = lax.axis_size(axis)
        ends = count - 1
        head = lax.slice_in_dim(cells, 0, width, axis=dim)
        tail = lax.slice_in_dim(cells, cells.shape[dim] - width, cells.shape[dim], axis=dim)
        cells = jnp.concatenate(
            [
                lax.ppermute(tail, axis, [(i, (i + 1) % count) for i in range(ends)]),
                cells,
                lax.ppermute(head, axis, [((i + 1) % count, i) for i in range(ends)]),
            ],
            axis=dim,
        )
    return cells


def taps_forward(padded, kernel, frame_count):
    summed = jnp.zeros((frame_count, padded.shape[1]), jnp.float32)
    for tap_index in range(kernel.shape[0]):
        summed = summed + kernel[tap_index] * padded[tap_index : tap_index + frame_count].astype(
            jnp.float32
        )
    return summed


def taps_backward(padded_grad, kernel, frame_count):
    reach_both = kernel.shape[0] - 1
    summed = jnp.zeros((frame_count, padded_grad.shape[1]), jnp.float32)
    for tap_index in range(kernel.shape[0]):
        begin = reach_both - tap_index
        summed = summed + kernel[tap_index] * padded_grad[begin : begin + frame_count].astype(
            jnp.float32
        )
    return summed


def taps_kernel(padded_glu, dconv_rows, kernel_taps, frame_count):
    grad_rows = dconv_rows.astype(jnp.float32)
    tap_rows = []
    for tap_index in range(kernel_taps):
        tap_rows.append(
            jnp.sum(
                padded_glu[tap_index : tap_index + frame_count].astype(jnp.float32) * grad_rows,
                axis=0,
            )
        )
    return jnp.stack(tap_rows)


def row_product(left_rows, right_mat, contract):
    dim_spec = (((1,), (contract,)), ((), ()))
    return lax.dot_general(left_rows, right_mat, dim_spec, preferred_element_type=jnp.float32)


def local(frames, lengths, w_in, w_dw, bn_gain, bn_bias, w_out, cotangent):
    frame_rows = frames.shape[1]
    channels = frames.shape[2]
    kernel_taps = w_dw.shape[0]
    reach = (kernel_taps - 1) // 2
    feats = frames[0]
    cot_rows = cotangent[0]
    tm_count = lax.axis_size("tm")
    device_count = lax.axis_size("dp") * tm_count
    offset = lax.axis_index("tm") * frame_rows
    limit = lengths[0]
    positions = offset + jnp.arange(frame_rows, dtype=jnp.int32)
    live_rows = (positions < limit).astype(jnp.float32)[:, None]
    contract_frames = (((0,), (0,)), ((), ()))
    pre_act = row_product(feats, w_in, 0)
    linear_half = pre_act[:, :channels]
    gate_sig = jax.nn.sigmoid(pre_act[:, channels:])
    glu_out = (linear_half * gate_sig * live_rows).astype(jnp.bfloat16)
    dswish = row_product(cot_rows, w_out, 1)
    padded = padded_2(glu_out, (("tm", 0),), reach)
    conv_out = taps_forward(padded, w_dw, frame_rows)
    local_sum = jnp.sum(conv_out * live_rows, axis=0)
    local_sq = jnp.sum(conv_out * conv_out * live_rows, axis=0)
    local_count = jnp.sum(live_rows)
    sums, squares, count = lax.psum((local_sum, local_sq, local_count), ("dp", "tm"))
    mean_vec = sums / count
    variance = squares / count - mean_vec * mean_vec
    inv_std = lax.rsqrt(variance + 1e-05)
    normed = (conv_out - mean_vec) * inv_std
    shifted = bn_gain * normed + bn_bias
    act_sig = jax.nn.sigmoid(shifted)
    swished = (shifted * act_sig * live_rows).astype(jnp.bfloat16)
    dshift = live_rows * dswish * act_sig * (1.0 + shifted * (1.0 - act_sig))
    sum_gain, sum_bias = lax.psum(
        (jnp.sum(dshift * normed, axis=0), jnp.sum(dshift, axis=0)), ("dp", "tm")
    )
    dconv = (
        live_rows * bn_gain * inv_std * (dshift - sum_bias / count - normed * sum_gain / count)
    ).astype(jnp.bfloat16)
    padded_grad = padded_2(dconv, (("tm", 0),), reach)
    dglu = live_rows * taps_backward(padded_grad, w_dw, frame_rows)
    kernel_sum = lax.psum(taps_kernel(padded, dconv, kernel_taps, frame_rows), ("dp", "tm"))
    out_rows = row_product(swished, w_out, 0).astype(jnp.bfloat16)
    dpre = jnp.concatenate(
        [dglu * gate_sig, dglu * linear_half * gate_sig * (1.0 - gate_sig)], axis=1
    ).astype(jnp.bfloat16)
    grad_rows = row_product(dpre, w_in, 1).astype(jnp.bfloat16)
    term_in = lax.dot_general(feats, dpre, contract_frames, preferred_element_type=jnp.float32)
    term_out = lax.dot_general(
        swished, cot_rows, contract_frames, preferred_element_type=jnp.float32
    )
    weight_term = jnp.concatenate([term_in, term_out], axis=1)
    weight_sum = lax.psum_scatter(weight_term, ("dp", "tm"), scatter_dimension=0, tiled=True)
    scale = 1.0 / math.sqrt(device_count * frame_rows)
    grad_w_in = weight_sum[:, : 2 * channels] * scale
    grad_w_out = weight_sum[:, 2 * channels :] * scale
    return (
        out_rows[None],
        grad_rows[None],
        grad_w_in,
        grad_w_out,
        kernel_sum * scale,
        sum_gain * scale,
        sum_bias * scale,
    )


def solution(mesh):
    placed = (P("dp", "tm", None), P("dp"), P(), P(), P(), P(), P(), P("dp", "tm", None))
    return jax.shard_map(
        local,
        mesh=mesh,
        in_specs=placed,
        out_specs=(
            P("dp", "tm", None),
            P("dp", "tm", None),
            P(("dp", "tm"), None),
            P(("dp", "tm"), None),
            P(),
            P(),
            P(),
        ),
        check_vma=False,
    )
```

profile of v0, /device:TPU:0, one launch (start us, length us, event | category | flops | bytes accessed | tf_op | source)
XLA Modules:
  0.0 603.7 jit_solution(6638876811179374699)
XLA Ops:
  8.0 5.7 fusion.143
  14.6 1.8 copy-done.4
  16.4 1.4 collective-permute-start
  17.8 1.3 collective-permute-start.1
  19.8 3.0 collective-permute-done.1
  22.8 24.4 %multiply_reduce_fusion.2 = (f32[1024]{0:T(1024)S(1)}, f32[1024]{0:T(1024)S(1)}, f32[768,1024]{1,0:T(8,128)}) fusion(f32[768]{0:T(1024)S(1)} %fusion.147, bf16[15,1024]{1,0:T(8,128)(2,1)S(1)} %collective-permute-done.1, bf16[768,1024]{1,0:T(8,128)(2,1)S(1)} %multiply_convert_fusion.4, f32[1024]{0:T(1024)S(1)} %bitcast.146, f32[1024]{0:T(1024)S(1)} %bitcast.148, ...), kind=kLoop, calls=%fused_computation.213 | loop fusion | flops 147060736 | bytes 4918272 | tf_op jit(solution)/shard_map/reduce_sum | solution.py:85
  47.2 69.6 %all-reduce.1 = (f32[1024]{0:T(1024)S(1)}, f32[]{:T(128)}, f32[1024]{0:T(1024)S(1)}) all-reduce(f32[1024]{0:T(1024)S(1)} %get-tuple-element.52, f32[]{:T(128)} %fusion.148, f32[1024]{0:T(1024)S(1)} %get-tuple-element.51), channel_id=1, replica_groups=mesh['dp'=16,'tm'=8] {'dp','tm'}, use_global_device_ids=true, to_apply=%region_5.0 | all-reduce | flops 2049 | bytes 16392 | tf_op jit(solution)/shard_map/psum | solution.py:88
  117.6 6.4 %fusion.151 = (f32[1024]{0:T(1024)S(1)}, f32[1024]{0:T(1024)S(1)}, f32[768,1024]{1,0:T(8,128)}) fusion(f32[1024]{0:T(1024)S(1)} %get-tuple-element.106, f32[768,1024]{1,0:T(8,128)} %get-tuple-element.67, f32[1024]{0:T(1024)S(1)} %get-tuple-element.105, f32[1024]{0:T(1024)S(1)} %copy-done.16, f32[1024]{0:T(1024)S(1)} %copy-done.12, ...), kind=kOutput, calls=%fused_computation.316 | convolution fusion | flops 1623193600 | bytes 9989120 | tf_op jit(solution)/shard_map/dot_general | solution.py:61
  124.0 63.8 %all-reduce = (f32[1024]{0:T(1024)S(1)}, f32[1024]{0:T(1024)S(1)}) all-reduce(f32[1024]{0:T(1024)S(1)} %get-tuple-element.58, f32[1024]{0:T(1024)S(1)} %get-tuple-element.57), channel_id=1, replica_groups=mesh['dp'=16,'tm'=8] {'dp','tm'}, use_global_device_ids=true, to_apply=%region_9.0 | all-reduce | flops 2048 | bytes 16384 | tf_op jit(solution)/shard_map/psum | solution.py:97
  187.8 1.2 broadcast_multiply_fusion.3
  189.0 15.0 %fusion.75 = (f32[1024]{0:T(1024)S(1)}, f32[1024]{0:T(1024)S(1)}, f32[1024]{0:T(1024)S(1)}, f32[1024]{0:T(1024)S(1)}, f32[1024]{0:T(1024)S(1)}, /*index=5*/f32[1024]{0:T(1024)S(1)}, bf16[768,1024]{1,0:T(8,128)(2,1)S(1)}) fusion(bf16[15,1024]{1,0:T(8,128)(2,1)S(1)} %collective-permute-done.1, bf16[768,1024]{1,0:T(8,128)(2,1)} %copy-done.1, ...), kind=kLoop, calls=%fused_computation.196 | loop fusion | flops 36956160 | bytes 9516036 | tf_op jit(solution)/shard_map/reduce_sum | solution.py:51
  204.1 1.3 collective-permute-start.2
  205.4 3.0 collective-permute-start.3
  208.4 2.7 fusion.60
  211.1 3.2 fusion.74
  214.4 2.9 fusion.59
  217.3 3.7 fusion.76
  221.0 4.5 fusion.139
  225.5 2.7 stack.127
  228.2 40.0 %multiply_convert_fusion.1 = (bf16[768,1024]{1,0:T(8,128)(2,1)S(1)}, f32[768,1024]{1,0:T(8,128)S(1)}) fusion(f32[768,2048]{1,0:T(8,128)} %copy-done.4, bf16[768,1024]{1,0:T(8,128)(2,1)} %copy-done.3, bf16[15,1024]{1,0:T(8,128)(2,1)S(1)} %collective-permute-done.3, f32[1024]{0:T(1024)S(1)} %bitcast.147, f32[1024]{0:T(1024)S(1)} %bitcast.149, ...), kind=kLoop, calls=%fused_computation.204 | loop fusion | flops 147849216 | bytes 9628672 | tf_op jit(solution)/shard_map/convert
  268.2 4.7 multiply_convert_fusion
  273.0 3.5 convolution_bitcast_fusion
  276.5 8.0 %pad_maximum_fusion = f32[1024,3072]{0,1:T(8,128)} fusion(f32[1024,1024]{0,1:T(8,128)S(1)} %copy-done.6, f32[1024,2048]{0,1:T(8,128)S(1)} %convolution_bitcast_fusion), kind=kLoop, calls=%fused_computation.32 | loop fusion | flops 3145728 | bytes 25165824 | tf_op jit(solution)/shard_map/concatenate | solution.py:115
  284.5 12.6 %copy.19 = f32[1024,3072]{1,0:T(8,128)} copy(f32[1024,3072]{0,1:T(8,128)} %pad_maximum_fusion) | data formatting | bytes 25165824
  297.7 5.4 fusion.146
  303.1 4.6 fusion.145
  307.6 58.1 %all-reduce.4.cloned.1.call-done = f32[31,1024]{1,0:T(8,128)} async-done(((f32[31,1024]{1,0:T(8,128)}), f32[31,1024]{1,0:T(8,128)}) %all-reduce.4.cloned.1.call-update) | async-done | bytes 126992 | tf_op jit(solution)/shard_map/psum | solution.py:105
  365.8 1.6 broadcast_multiply_fusion.2
  367.4 223.3 %reduce-scatter.4.cloned.1.call-done = f32[8,3072]{1,0:T(8,128)} async-done(((f32[1024,3072]{1,0:T(8,128)}), f32[8,3072]{1,0:T(8,128)}) %reduce-scatter.4.cloned.1.call-update) | async-done | bytes 98320
  592.4 0.8 slice.635
  593.6 1.1 broadcast_multiply_fusion
  594.7 2.2 copy.17
  (54 shorter events, 5.1 us)
Async XLA Ops:
  7.2 110.4 %copy-start = (bf16[1024,1024]{1,0:T(8,128)(2,1)S(1)}, bf16[1024,1024]{1,0:T(8,128)(2,1)}, u32[]{:S(2)}) copy-start(bf16[1024,1024]{1,0:T(8,128)(2,1)} %param.14) | copy-start | bytes 6291460
  7.2 358.6 %all-reduce.4.cloned.1.call-start = ((), (), s32[]{:S(2)}) async-start(), calls=%async_computation.1 | async-start | bytes 262144 | tf_op jit(solution)/shard_map/psum | solution.py:105
  13.7 2.7 copy-start.4
  13.7 5.4 copy-start.11
  16.4 6.4 %copy-start.1 = (bf16[768,1024]{1,0:T(8,128)(2,1)}, bf16[768,1024]{1,0:T(8,128)(2,1)S(1)}, u32[]{:S(2)}) copy-start(bf16[768,1024]{1,0:T(8,128)(2,1)S(1)} %multiply_convert_fusion.4) | copy-start | bytes 4718596
  16.4 101.2 %copy-start.12 = (f32[1024]{0:T(1024)S(1)}, f32[1024]{0:T(1024)}, u32[]{:S(2)}) copy-start(f32[1024]{0:T(1024)} %param.12) | copy-start | bytes 12292
  16.4 101.2 %copy-start.16 = (f32[1024]{0:T(1024)S(1)}, f32[1024]{0:T(1024)}, u32[]{:S(2)}) copy-start(f32[1024]{0:T(1024)} %param.13) | copy-start | bytes 12292
  16.4 3.5 collective-permute-start
  17.8 5.0 collective-permute-start.1
  189.0 19.4 %copy-start.2 = (bf16[768,1024]{1,0:T(8,128)(2,1)S(1)}, bf16[768,1024]{1,0:T(8,128)(2,1)}, u32[]{:S(2)}) copy-start(bf16[768,1024]{1,0:T(8,128)(2,1)} %copy-done.1) | copy-start | bytes 4718596
  204.0 13.2 %copy-start.3 = (bf16[768,1024]{1,0:T(8,128)(2,1)}, bf16[768,1024]{1,0:T(8,128)(2,1)S(1)}, u32[]{:S(2)}) copy-start(bf16[768,1024]{1,0:T(8,128)(2,1)S(1)} %get-tuple-element.64) | copy-start | bytes 4718596
  204.1 24.1 %collective-permute-start.2 = (bf16[15,1024]{1,0:T(8,128)(2,1)S(1)}, bf16[15,1024]{1,0:T(8,128)(2,1)S(1)}, u32[]{:S(2)}, u32[]{:S(2)}) collective-permute-start(bf16[15,1024]{1,0:T(8,128)(2,1)S(1)} %get-tuple-element.68), channel_id=1, source_target_pairs={{1,0},{2,1},{3,2},{4,3},{5,4},{6,5},{7,6},{9,8},{10,9},{11,10},{12... | collective-permute-start | bytes 92168 | tf_op jit(solution)/shard_map/ppermute | solution.py:19
  205.4 22.8 %collective-permute-start.3 = (bf16[15,1024]{1,0:T(8,128)(2,1)S(1)}, bf16[15,1024]{1,0:T(8,128)(2,1)S(1)}, u32[]{:S(2)}, u32[]{:S(2)}) collective-permute-start(bf16[15,1024]{1,0:T(8,128)(2,1)S(1)} %get-tuple-element.69), channel_id=1, source_target_pairs={{0,1},{1,2},{2,3},{3,4},{4,5},{5,6},{6,7},{8,9},{9,10},{10,11},{11... | collective-permute-start | bytes 92168 | tf_op jit(solution)/shard_map/ppermute | solution.py:17
  214.3 6.6 %copy-start.5 = (f32[768,1024]{1,0:T(8,128)S(1)}, f32[768,1024]{1,0:T(8,128)}, u32[]{:S(2)}) copy-start(f32[768,1024]{1,0:T(8,128)} %get-tuple-element.67) | copy-start | bytes 9437188
  214.3 6.6 %copy-start.14 = (bf16[1,768,1024]{2,1,0:T(8,128)(2,1)S(1)}, bf16[1,768,1024]{2,1,0:T(8,128)(2,1)}, u32[]{:S(2)}) copy-start(bf16[1,768,1024]{2,1,0:T(8,128)(2,1)} %param.15) | copy-start | bytes 4718596
  228.1 362.5 %reduce-scatter.4.cloned.1.call-start = ((), (), s32[]{:S(2)}) async-start(), calls=%async_computation.2 | async-start | bytes 12681216
  268.2 4.7 copy-start.7
  268.2 4.7 copy-start.15
  272.9 3.5 copy-start.9
  272.9 3.5 copy-start.6
  297.7 5.4 copy-start.8
  297.7 5.4 copy-start.10
  297.7 5.4 copy-start.13
Sparse Core Ops, SparseCore 0:
  228.3 137.4 all-reduce.3
  371.5 219.0 reduce-scatter.3
where the time goes:
time: 604 us
  waiting for transfers between devices  284 us (47%)
  blocking collectives  133 us (22%)
  other arithmetic  111 us (18%)
  matrix products  30 us (5%)
  local copies, waits for them, and re-layouts  22.3 us (4%)
  between operations  15.2 us (3%)
  starting transfers between devices  7.12 us (1%)
    unnamed x3, waiting for transfers between devices  223 us
    psum x1, blocking collectives, local(): lax.psum((local_sum, local_sq, local_count), ('dp', 'tm'))  69.6 us
    psum x1, blocking collectives, local(): lax.psum((jnp.sum(dshift * normed, axis=0), jnp.sum(dshift, axis=0)), ('d...  63.8 us
    psum x1, waiting for transfers between devices, local(): lax.psum(taps_kernel(padded, dconv, kernel_taps, frame_rows), ('dp', 'tm'))  58.1 us
    another operation x2, other arithmetic  44.7 us
    reduce_sum x5, other arithmetic, taps_kernel(): jnp.sum(padded_glu[tap_index:tap_index + frame_count].astype(jnp.float32)...  27.5 us
    reduce_sum x1, other arithmetic, local(): local_sum = jnp.sum(conv_out * live_rows, axis=0)  24.4 us
    dot_general x4, matrix products, row_product(): lax.dot_general(left_rows, right_mat, dim_spec, preferred_element_type=jn...  22 us
  transfers between devices with their start and end apart: 6, of which 3 were waited for; matrix products, arithmetic and copies ran while one was open for 17% of the time, Pallas kernels for 0%

commit v1 on v0

v1 whole, which is shorter than its diff:
```python
import math

import jax
import jax.numpy as jnp
from jax import lax
from jax.experimental import pallas as pl
from jax.experimental.pallas import tpu as pltpu
from jax.sharding import PartitionSpec as P

MESH_ID = pl.DeviceIdType.MESH
F32 = jnp.float32
BF16 = jnp.bfloat16

ROWS = 768
CH = 1024
CB = 8
PAD = 16
PROWS = ROWS + 2 * PAD
TAPS = 31
COUNT = 58982.0
NDP, NTM = 16, 8
GRP = 8
GROUPS = ROWS // (8 * GRP)
MB = 256
NB = 6
ORDERS = (("z", "x", "y"), ("x", "y", "z"), ("y", "z", "x"))


def sigmoid(x):
    return 0.5 * jnp.tanh(0.5 * x) + 0.5


def dot_nn(a, b):
    return lax.dot_general(a, b, (((1,), (0,)), ((), ())), preferred_element_type=F32)


def dot_nt(a, b):
    return lax.dot_general(a, b, (((1,), (1,)), ((), ())), preferred_element_type=F32)


def kernel(
    len_ref, frames_h, w_in_h, w_dw, gain_ref, bias_ref, w_out_h, cot_h,
    out_h, gf_h, gwi_ref, gwo_ref, gk_ref, gg_ref, gb_ref,
    feats, w_in, w_out, cot, featsT, lin_v, sig_v, glu_p, dcv_p, conv_v, dsh_v,
    sw_v, swT, dpre_v, out_v, wb, vec,
    red, red_in, red_mid, red_rx1, red_rx2,
    gkl, kr1, ks1, kr2, kfull,
    wl, crx, cs, r1, s1, r2, s2, r3,
    in_sem, out_sem, halo_s, halo_r, ar1_s, ar1_r, ar2_s, ar2_r,
    k1_s, k1_r, k2_s, k2_r, k3_s, k3_r, rs_s, rs_r,
):
    dp = lax.axis_index("dp")
    tm = lax.axis_index("tm")
    z, x = dp // 4, dp % 4
    y, core = tm // 2, tm % 2
    pos = {"z": z, "x": x, "y": y}

    def at_axis(axis, p):
        if axis == "z":
            return (p * 4 + x, tm)
        if axis == "x":
            return (z * 4 + p, tm)
        return (dp, p * 2 + core)

    def rcopy(src, dst, ss, rs, dev):
        return pltpu.make_async_remote_copy(
            src_ref=src, dst_ref=dst, send_sem=ss, recv_sem=rs,
            device_id=dev, device_id_type=MESH_ID,
        )

    loads = [
        pltpu.make_async_copy(frames_h, feats, in_sem.at[0]),
        pltpu.make_async_copy(w_in_h, w_in, in_sem.at[1]),
        pltpu.make_async_copy(cot_h, cot, in_sem.at[2]),
        pltpu.make_async_copy(w_out_h, w_out, in_sem.at[3]),
    ]
    for c in loads:
        c.start()
    barrier = pltpu.get_barrier_semaphore()
    for d in range(1, NTM):
        pl.semaphore_signal(barrier, inc=1, device_id=(dp, (tm + d) % NTM), device_id_type=MESH_ID)
    for d in range(1, NDP):
        pl.semaphore_signal(barrier, inc=1, device_id=((dp + d) % NDP, tm), device_id_type=MESH_ID)

    limit = len_ref[0] - tm * ROWS

    def live_of(row0, rows, cols):
        t = lax.broadcasted_iota(jnp.int32, (rows, cols), 0) + row0
        return t < limit

    @pl.loop(0, TAPS)
    def _(k):
        row = w_dw[pl.ds(k, 1), :]
        for cb in range(CB):
            wb[cb, k + 1] = jnp.broadcast_to(row[:, cb * 128 : cb * 128 + 128], (8, 128))

    for ref in (glu_p, dcv_p):
        @pl.when(tm == 0)
        def _():
            ref[:, 0:PAD, :] = jnp.zeros((CB, PAD, 128), F32)

        @pl.when(tm == NTM - 1)
        def _():
            ref[:, PAD + ROWS : PROWS, :] = jnp.zeros((CB, PAD, 128), F32)

    loads[0].wait()
    loads[1].wait()

    @pl.loop(0, 4)
    def _(j):
        c0 = pl.multiple_of(j * 256, 256)

        @pl.loop(0, ROWS // MB)
        def _(m):
            r0 = pl.multiple_of(m * MB, MB)
            rows = feats[pl.ds(r0, MB), :]
            lin = dot_nn(rows, w_in[:, pl.ds(c0, 256)])
            sig = sigmoid(dot_nn(rows, w_in[:, pl.ds(CH + c0, 256)]))
            glu = jnp.where(live_of(r0, MB, 256), lin * sig, 0.0).astype(BF16).astype(F32)
            for h in range(2):
                cols = slice(h * 128, h * 128 + 128)
                lin_v[2 * j + h, pl.ds(r0, MB), :] = lin[:, cols]
                sig_v[2 * j + h, pl.ds(r0, MB), :] = sig[:, cols]
                glu_p[2 * j + h, pl.ds(PAD + r0, MB), :] = glu[:, cols]

    pl.semaphore_wait(barrier, NTM + NDP - 2)

    def halo(ref, n):
        to_left = rcopy(
            ref.at[:, pl.ds(PAD, PAD), :], ref.at[:, pl.ds(PAD + ROWS, PAD), :],
            halo_s.at[n], halo_r.at[n], (dp, (tm + NTM - 1) % NTM),
        )
        to_right = rcopy(
            ref.at[:, pl.ds(ROWS, PAD), :], ref.at[:, pl.ds(0, PAD), :],
            halo_s.at[n + 1], halo_r.at[n + 1], (dp, (tm + 1) % NTM),
        )

        def start():
            pl.when(tm > 0)(to_left.start)
            pl.when(tm < NTM - 1)(to_right.start)

        def recv():
            pl.when(tm < NTM - 1)(to_left.wait_recv)
            pl.when(tm > 0)(to_right.wait_recv)

        def sent():
            pl.when(tm > 0)(to_left.wait_send)
            pl.when(tm < NTM - 1)(to_right.wait_send)

        return start, recv, sent

    halo_g, halo_d = halo(glu_p, 0), halo(dcv_p, 2)
    halo_g[0]()

    loads[2].wait()
    loads[3].wait()

    @pl.loop(0, 4)
    def _(j):
        c0 = pl.multiple_of(j * 256, 256)

        @pl.loop(0, ROWS // MB)
        def _(m):
            r0 = pl.multiple_of(m * MB, MB)
            ds = dot_nt(cot[pl.ds(r0, MB), :], w_out[pl.ds(c0, 256), :])
            for h in range(2):
                dsh_v[2 * j + h, pl.ds(r0, MB), :] = ds[:, h * 128 : h * 128 + 128]

    def taps_pass(src, cb, row0, tap_of):
        acc = [None] * GRP
        for r in range(8):
            xs = [src[cb, pl.ds(row0 + (8 * n + r), 8), :] for n in range(GRP + 3)]
            for q in range(4):
                o = 8 * q + r
                if o == 0:
                    continue
                w = wb[cb, tap_of(o)]
                for g in range(GRP):
                    term = w * xs[g + q]
                    acc[g] = term if acc[g] is None else acc[g] + term
        return acc

    halo_g[1]()

    @pl.loop(0, CB)
    def _(cb):
        def step(i, carry):
            row0 = pl.multiple_of(i * (8 * GRP), 8 * GRP)
            s, sq = carry
            acc = taps_pass(glu_p, cb, row0, lambda o: o)
            for g in range(GRP):
                conv_v[cb, pl.ds(row0 + 8 * g, 8), :] = acc[g]
                kept = jnp.where(live_of(row0 + 8 * g, 8, 128), acc[g], 0.0)
                s = s + kept
                sq = sq + kept * kept
            return s, sq

        zero = jnp.zeros((8, 128), F32)
        s, sq = lax.fori_loop(0, GROUPS, step, (zero, zero))
        red[0, pl.ds(cb, 1), :] = jnp.sum(s, axis=0, keepdims=True)
        red[1, pl.ds(cb, 1), :] = jnp.sum(sq, axis=0, keepdims=True)

    def spread(axis, count, src_of, dst, ss, rs):
        me = tm if axis == "tm" else dp

        def copy(d, slot):
            peer = (me + d) % count
            dev = (dp, peer) if axis == "tm" else (peer, tm)
            return rcopy(src_of(peer), dst.at[slot], ss.at[d], rs.at[slot], dev)

        def start():
            for d in range(1, count):
                copy(d, me).start()

        def recv():
            for d in range(1, count):
                copy(d, (me + d) % count).wait_recv()

        def sent():
            for d in range(1, count):
                copy(d, me).wait_send()

        return start, recv, sent

    def total(ref, count):
        acc = ref[0]
        for i in range(1, count):
            acc = acc + ref[i]
        return acc

    def all_sum(n):
        one = spread("tm", NTM, lambda p: red_in.at[n], red_rx1.at[n], ar1_s.at[n], ar1_r.at[n])
        two = spread("dp", NDP, lambda p: red_mid.at[n], red_rx2.at[n], ar2_s.at[n], ar2_r.at[n])

        def begin():
            v = red[...]
            red_in[n] = v
            red_rx1[n, tm] = v
            one[0]()

        def middle():
            one[1]()
            v = total(red_rx1.at[n], NTM)
            red_mid[n] = v
            red_rx2[n, dp] = v
            two[0]()

        def end():
            two[1]()
            return total(red_rx2.at[n], NDP)

        def sent():
            one[2]()
            two[2]()

        return begin, middle, end, sent

    ar_a, ar_b = all_sum(0), all_sum(1)
    ar_a[0]()

    @pl.loop(0, 4)
    def _(i):
        c0 = pl.multiple_of(i * 256, 256)
        featsT[pl.ds(c0, 256), :] = feats[:, pl.ds(c0, 256)].T

    ar_a[1]()
    sums = ar_a[2]()
    mean = sums[0] * (1.0 / COUNT)
    variance = sums[1] * (1.0 / COUNT) - mean * mean
    inv_std = lax.rsqrt(variance + 1e-05)
    vec[0] = mean
    vec[1] = inv_std
    vec[2] = gain_ref[...]
    vec[3] = bias_ref[...]

    @pl.loop(0, CB)
    def _(cb):
        mean_r = vec[0, pl.ds(cb, 1), :]
        inv_r = vec[1, pl.ds(cb, 1), :]
        gain_r = vec[2, pl.ds(cb, 1), :]
        bias_r = vec[3, pl.ds(cb, 1), :]

        def step(i, carry):
            sg, sb = carry
            n = 64
            row0 = pl.multiple_of(i * n, n)
            live = live_of(row0, n, 128)
            normed = (conv_v[cb, pl.ds(row0, n), :] - mean_r) * inv_r
            shifted = gain_r * normed + bias_r
            act = sigmoid(shifted)
            sw_v[cb, pl.ds(row0, n), :] = jnp.where(live, shifted * act, 0.0).astype(BF16)
            slope = act * (1.0 + shifted * (1.0 - act))
            dsh = jnp.where(live, dsh_v[cb, pl.ds(row0, n), :] * slope, 0.0)
            dsh_v[cb, pl.ds(row0, n), :] = dsh
            conv_v[cb, pl.ds(row0, n), :] = normed
            prod = dsh * normed
            for g in range(n // 8):
                sg = sg + prod[8 * g : 8 * g + 8]
                sb = sb + dsh[8 * g : 8 * g + 8]
            return sg, sb

        zero = jnp.zeros((8, 128), F32)
        sg, sb = lax.fori_loop(0, ROWS // 64, step, (zero, zero))
        red[0, pl.ds(cb, 1), :] = jnp.sum(sg, axis=0, keepdims=True)
        red[1, pl.ds(cb, 1), :] = jnp.sum(sb, axis=0, keepdims=True)

    ar_b[0]()

    @pl.loop(0, ROWS // MB)
    def _(m):
        r0 = pl.multiple_of(m * MB, MB)
        rows = jnp.concatenate([sw_v[cb, pl.ds(r0, MB), :] for cb in range(CB)], axis=1)

        @pl.loop(0, 4)
        def _(j):
            c0 = pl.multiple_of(j * 256, 256)
            out_v[0, pl.ds(r0, MB), pl.ds(c0, 256)] = dot_nn(rows, w_out[:, pl.ds(c0, 256)]).astype(BF16)

    out_copy = pltpu.make_async_copy(out_v.at[0], out_h, out_sem.at[0])
    out_copy.start()
    ar_b[1]()

    def put_terms(b, i, first, second):
        both = jnp.concatenate(
            [first.reshape(16, 2, 8, 256), second.reshape(16, 2, 8, 256)], axis=2
        )
        wl[b, pl.ds(16 * i, 16)] = both.astype(BF16)

    def rs_core(b):
        return rcopy(
            wl.at[b, :, 1 - core], crx.at[b], rs_s.at[b, 0], rs_r.at[b, 0],
            (dp, tm + 1 - 2 * core),
        )

    def part_of(ref, dims, axis, p):
        at = dims.index(axis)
        return ref.at[tuple(slice(None) for _ in range(at)) + (p,)]

    def rs_copies(b, stage):
        order = ORDERS[b % 3]
        dims = ("z", "x", "y")
        src, dst = ((cs, r1), (s1, r2), (s2, r3))[stage]
        dims = tuple(a for a in dims if a not in order[:stage])
        axis = order[stage]
        copies = []
        for d in range(1, 4):
            p = (pos[axis] + d) % 4
            copies.append(
                rcopy(
                    part_of(src.at[b], dims, axis, p), dst.at[b, d - 1],
                    rs_s.at[b, 3 * stage + d], rs_r.at[b, 3 * stage + d], at_axis(axis, p),
                )
            )
        own = part_of(src.at[b], dims, axis, pos[axis])
        return copies, own, dst.at[b]

    def rs_one(b):
        rs_core(b).wait_recv()

        @pl.loop(0, 4)
        def _(i):
            rows = pl.ds(i * 16, 16)
            both = wl[b, rows, core].astype(F32) + crx[b, rows].astype(F32)
            cs[b, i] = both.astype(BF16).reshape(4, 4, 16, 256)

        for c in rs_copies(b, 0)[0]:
            c.start()

    def rs_next(b, stage):
        copies, own, got = rs_copies(b, stage)
        for c in copies:
            c.wait_recv()
        acc = own[...].astype(F32)
        for d in range(3):
            acc = acc + got[d].astype(F32)
        if stage < 2:
            (s1, s2)[stage][b] = acc.astype(BF16)
            for c in rs_copies(b, stage + 1)[0]:
                c.start()
        else:
            acc = acc * SCALE
            if b < 2:
                gwo_ref[:, 512 * b : 512 * b + 256] = acc[0:8]
                gwo_ref[:, 512 * b + 256 : 512 * b + 512] = acc[8:16]
            else:
                j = b - 2
                gwi_ref[:, 256 * j : 256 * j + 256] = acc[0:8]
                gwi_ref[:, CH + 256 * j : CH + 256 * j + 256] = acc[8:16]

    @pl.loop(0, 4)
    def _(i):
        for h in range(2):
            swT[pl.ds(256 * i + 128 * h, 128), :] = sw_v[2 * i + h].T

    for b in range(2):
        @pl.loop(0, 4)
        def _(i):
            rows = swT[pl.ds(pl.multiple_of(256 * i, 256), 256), :]
            put_terms(
                b, i,
                dot_nn(rows, cot[:, 512 * b : 512 * b + 256]),
                dot_nn(rows, cot[:, 512 * b + 256 : 512 * b + 512]),
            )

        rs_core(b).start()

    grads = ar_b[2]()
    gg_ref[...] = grads[0] * SCALE
    gb_ref[...] = grads[1] * SCALE
    vec[4] = gain_ref[...] * vec[1]
    vec[5] = grads[1] * (1.0 / COUNT)
    vec[6] = grads[0] * (1.0 / COUNT)

    @pl.loop(0, CB)
    def _(cb):
        factor = vec[4, pl.ds(cb, 1), :]
        shift = vec[5, pl.ds(cb, 1), :]
        tilt = vec[6, pl.ds(cb, 1), :]

        @pl.loop(0, ROWS // 64)
        def _(i):
            n = 64
            row0 = pl.multiple_of(i * n, n)
            inner = dsh_v[cb, pl.ds(row0, n), :] - shift - conv_v[cb, pl.ds(row0, n), :] * tilt
            dcv = jnp.where(live_of(row0, n, 128), factor * inner, 0.0)
            dcv_p[cb, pl.ds(PAD + row0, n), :] = dcv.astype(BF16).astype(F32)

    halo_d[0]()
    rs_one(0)
    rs_one(1)

    @pl.loop(0, CB)
    def _(cb):
        def step(i, accs):
            row0 = pl.multiple_of(i * (8 * GRP), 8 * GRP)
            accs = list(accs)
            ds = [dcv_p[cb, pl.ds(row0 + PAD + 8 * g, 8), :] for g in range(GRP)]
            for r in range(8):
                xs = [glu_p[cb, pl.ds(row0 + (8 * n + r), 8), :] for n in range(GRP + 3)]
                for q in range(4):
                    o = 8 * q + r
                    if o == 0:
                        continue
                    for g in range(GRP):
                        accs[o - 1] = accs[o - 1] + xs[g + q] * ds[g]
            return tuple(accs)

        zero = jnp.zeros((8, 128), F32)
        accs = lax.fori_loop(0, GROUPS, step, (zero,) * TAPS)
        for k in range(TAPS):
            gkl[k, pl.ds(cb, 1), :] = jnp.sum(accs[k], axis=0, keepdims=True)

    gkl[TAPS] = jnp.zeros((8, 128), F32)

    kt1 = spread("tm", NTM, lambda p: gkl.at[pl.ds(4 * p, 4)], kr1, k1_s, k1_r)
    kt2 = spread("dp", NDP, lambda p: ks1.at[0], kr2, k2_s, k2_r)
    kt3 = spread("tm", NTM, lambda p: ks1.at[1], kfull, k3_s, k3_r)
    kr1[tm] = gkl[pl.ds(4 * tm, 4)]
    kt1[0]()
    halo_d[1]()

    def back_block(j):
        b = 2 + j
        for h in range(2):
            cb = 2 * j + h

            @pl.loop(0, GROUPS)
            def _(i):
                row0 = pl.multiple_of(i * (8 * GRP), 8 * GRP)
                acc = taps_pass(dcv_p, cb, row0, lambda o: 32 - o)
                for g in range(0, GRP, 2):
                    dl, dg = [], []
                    for e in (g, g + 1):
                        rows = pl.ds(row0 + 8 * e, 8)
                        dglu = jnp.where(live_of(row0 + 8 * e, 8, 128), acc[e], 0.0)
                        sig = sig_v[cb, rows, :]
                        half = dglu * sig
                        dl.append(half)
                        dg.append(half * lin_v[cb, rows, :] * (1.0 - sig))
                    rows = pl.ds(row0 + 8 * g, 16)
                    dpre_v[cb, rows, :] = jnp.concatenate(dl, axis=0).astype(BF16)
                    dpre_v[CB + cb, rows, :] = jnp.concatenate(dg, axis=0).astype(BF16)

        first = jnp.concatenate([dpre_v[2 * j], dpre_v[2 * j + 1]], axis=1)
        second = jnp.concatenate([dpre_v[CB + 2 * j], dpre_v[CB + 2 * j + 1]], axis=1)

        @pl.loop(0, 4)
        def _(i):
            rows = featsT[pl.ds(pl.multiple_of(256 * i, 256), 256), :]
            put_terms(b, i, dot_nn(rows, first), dot_nn(rows, second))

        rs_core(b).start()

    back_block(0)
    rs_next(0, 0)
    rs_next(1, 0)
    kt1[1]()
    v = total(kr1, NTM)
    ks1[0] = v
    kr2[dp] = v
    kt2[0]()
    back_block(1)
    rs_one(2)
    rs_next(0, 1)
    rs_next(1, 1)
    kt2[1]()
    v = total(kr2, NDP)
    ks1[1] = v
    kfull[tm] = v
    kt3[0]()
    back_block(2)
    rs_one(3)
    rs_next(2, 0)
    rs_next(0, 2)
    rs_next(1, 2)
    kt3[1]()
    for cb in range(CB):
        for k in range(TAPS):
            gk_ref[k : k + 1, 128 * cb : 128 * cb + 128] = kfull[k // 4, k % 4, cb : cb + 1, :] * SCALE
    back_block(3)
    rs_one(4)
    rs_next(3, 0)
    rs_next(2, 1)

    def frame_rows(m):
        r0 = MB * m
        rows = jnp.concatenate([dpre_v[c, pl.ds(r0, MB), :] for c in range(2 * CB)], axis=1)

        @pl.loop(0, 4)
        def _(j):
            c0 = pl.multiple_of(j * 256, 256)
            out_v[1, pl.ds(r0, MB), pl.ds(c0, 256)] = dot_nt(rows, w_in[pl.ds(c0, 256), :]).astype(BF16)

    frame_rows(0)
    rs_one(5)
    rs_next(4, 0)
    rs_next(3, 1)
    rs_next(2, 2)
    frame_rows(1)
    rs_next(5, 0)
    rs_next(4, 1)
    rs_next(3, 2)
    frame_rows(2)
    gf_copy = pltpu.make_async_copy(out_v.at[1], gf_h, out_sem.at[1])
    gf_copy.start()
    rs_next(5, 1)
    rs_next(4, 2)
    rs_next(5, 2)

    for t in (halo_g, halo_d, kt1, kt2, kt3):
        t[2]()
    ar_a[3]()
    ar_b[3]()
    for b in range(NB):
        rs_core(b).wait_send()
        for stage in range(3):
            for c in rs_copies(b, stage)[0]:
                c.wait_send()
    out_copy.wait()
    gf_copy.wait()


SCALE = 1.0 / math.sqrt(16 * 6144)


def local(frames, lengths, w_in, w_dw, bn_gain, bn_bias, w_out, cotangent):
    hbm = pl.BlockSpec(memory_space=pl.ANY)
    vmem = pl.BlockSpec(memory_space=pltpu.VMEM)
    smem = pl.BlockSpec(memory_space=pltpu.SMEM)
    dma = pltpu.SemaphoreType.DMA
    outs = pl.pallas_call(
        kernel,
        out_shape=(
            jax.ShapeDtypeStruct((ROWS, CH), BF16),
            jax.ShapeDtypeStruct((ROWS, CH), BF16),
            jax.ShapeDtypeStruct((8, 2 * CH), F32),
            jax.ShapeDtypeStruct((8, CH), F32),
            jax.ShapeDtypeStruct((TAPS, CH), F32),
            jax.ShapeDtypeStruct((8, 128), F32),
            jax.ShapeDtypeStruct((8, 128), F32),
        ),
        in_specs=[smem, hbm, hbm, vmem, vmem, vmem, hbm, hbm],
        out_specs=(hbm, hbm, vmem, vmem, vmem, vmem, vmem),
        scratch_shapes=[
            pltpu.VMEM((ROWS, CH), BF16),
            pltpu.VMEM((CH, 2 * CH), BF16),
            pltpu.VMEM((CH, CH), BF16),
            pltpu.VMEM((ROWS, CH), BF16),
            pltpu.VMEM((CH, ROWS), BF16),
            pltpu.VMEM((CB, ROWS, 128), F32),
            pltpu.VMEM((CB, ROWS, 128), F32),
            pltpu.VMEM((CB, PROWS, 128), F32),
            pltpu.VMEM((CB, PROWS, 128), F32),
            pltpu.VMEM((CB, ROWS, 128), F32),
            pltpu.VMEM((CB, ROWS, 128), F32),
            pltpu.VMEM((CB, ROWS, 128), BF16),
            pltpu.VMEM((CH, ROWS), BF16),
            pltpu.VMEM((2 * CB, ROWS, 128), BF16),
            pltpu.VMEM((2, ROWS, CH), BF16),
            pltpu.VMEM((CB, 32, 8, 128), F32),
            pltpu.VMEM((8, 8, 128), F32),
            pltpu.VMEM((2, 8, 128), F32),
            pltpu.VMEM((2, 2, 8, 128), F32),
            pltpu.VMEM((2, 2, 8, 128), F32),
            pltpu.VMEM((2, NTM, 2, 8, 128), F32),
            pltpu.VMEM((2, NDP, 2, 8, 128), F32),
            pltpu.VMEM((32, 8, 128), F32),
            pltpu.VMEM((NTM, 4, 8, 128), F32),
            pltpu.VMEM((2, 4, 8, 128), F32),
            pltpu.VMEM((NDP, 4, 8, 128), F32),
            pltpu.VMEM((NTM, 4, 8, 128), F32),
            pltpu.VMEM((NB, 64, 2, 16, 256), BF16),
            pltpu.VMEM((NB, 64, 16, 256), BF16),
            pltpu.VMEM((NB, 4, 4, 4, 16, 256), BF16),
            pltpu.VMEM((NB, 3, 4, 4, 16, 256), BF16),
            pltpu.VMEM((NB, 4, 4, 16, 256), BF16),
            pltpu.VMEM((NB, 3, 4, 16, 256), BF16),
            pltpu.VMEM((NB, 4, 16, 256), BF16),
            pltpu.VMEM((NB, 3, 16, 256), BF16),
            dma((4,)),
            dma((2,)),
            dma((4,)),
            dma((4,)),
            dma((2, NTM)),
            dma((2, NTM)),
            dma((2, NDP)),
            dma((2, NDP)),
            dma((NTM,)),
            dma((NTM,)),
            dma((NDP,)),
            dma((NDP,)),
            dma((NTM,)),
            dma((NTM,)),
            dma((NB, 10)),
            dma((NB, 10)),
        ],
        compiler_params=pltpu.CompilerParams(
            collective_id=0, has_side_effects=True, vmem_limit_bytes=62 << 20
        ),
        name="conformer_conv",
    )(
        lengths, frames[0], w_in, w_dw, bn_gain.reshape(8, 128), bn_bias.reshape(8, 128),
        w_out, cotangent[0],
    )
    out, gf, gwi, gwo, gk, gg, gb = outs
    return (out[None], gf[None], gwi, gwo, gk, gg.reshape(CH), gb.reshape(CH))


def solution(mesh):
    placed = (P("dp", "tm", None), P("dp"), P(), P(), P(), P(), P(), P("dp", "tm", None))
    return jax.shard_map(
        local,
        mesh=mesh,
        in_specs=placed,
        out_specs=(
            P("dp", "tm", None),
            P("dp", "tm", None),
            P(("dp", "tm"), None),
            P(("dp", "tm"), None),
            P(),
            P(),
            P(),
        ),
        check_vma=False,
    )
```

time: 604 us -> 111 us (0.18)
  waiting for transfers between devices: 284 us -> 0 us
  blocking collectives: 133 us -> 0 us
  other arithmetic: 111 us -> 0 us
  Pallas kernels: 0 us -> 102 us
  matrix products: 30 us -> 0 us
  local copies, waits for them, and re-layouts: 22.3 us -> 7.04 us
  between operations: 15.2 us -> 1.32 us
  starting transfers between devices: 7.12 us -> 0 us
    unnamed x3 -> x0, waiting for transfers between devices: 223 us -> none
    psum x2 -> x0, blocking collectives: 133 us -> none  [the longest x1 69.6 us: local(): lax.psum((local_sum, local_sq, local_count), ('dp', 'tm'))]
    pallas_call x0 -> x1, Pallas kernels: none -> 102 us  [local(): pl.pallas_call(kernel, out_shape=(jax.ShapeDtypeStruct((ROWS, CH), BF16),...]
    psum x1 -> x0, waiting for transfers between devices: 58.1 us -> none  [local(): lax.psum(taps_kernel(padded, dconv, kernel_taps, frame_rows), ('dp', 'tm'))]
    reduce_sum x7 -> x0, other arithmetic: 52.5 us -> none  [the longest x5 27.5 us: taps_kernel(): jnp.sum(padded_glu[tap_index:tap_index + frame_count].astype(jnp.float32)...]
    another operation x2 -> x0, other arithmetic: 44.7 us -> none
    dot_general x6 -> x0, matrix products: 30 us -> none  [the longest x4 22 us: row_product(): lax.dot_general(left_rows, right_mat, dim_spec, preferred_element_type=jn...]
    unnamed x39 -> x19, local copies, waits for them, and re-layouts: 17.9 us -> 7.04 us
  transfers between devices with their start and end apart: 6 -> 0, of which waited for: 3 -> 0; matrix products, arithmetic and copies ran while one was open for 17% -> 0% of each run, Pallas kernels for 0% -> 0%
where the time goes in v1:
time: 111 us
  Pallas kernels  102 us (92%)
  local copies, waits for them, and re-layouts  7.04 us (6%)
  between operations  1.32 us (1%)
    pallas_call x1, Pallas kernels, local(): pl.pallas_call(kernel, out_shape=(jax.ShapeDtypeStruct((ROWS, CH), BF16),...  102 us
    unnamed x19, local copies, waits for them, and re-layouts  7.04 us

profile of v1, /device:TPU:0, one launch (start us, length us, event | category | flops | bytes accessed | tf_op | source)
XLA Modules:
  0.0 110.8 jit_solution(784973158956844604)
XLA Ops:
  1.3 102.4 %conformer_conv.1 = (bf16[768,1024]{1,0:T(8,128)(2,1)}, bf16[768,1024]{1,0:T(8,128)(2,1)}, f32[8,2048]{1,0:T(8,128)}, f32[8,1024]{1,0:T(8,128)}, f32[31,1024]{1,...) custom-call(s32[1]{0:T(128)S(6)} %copy.22.len_ref, bf16[768,1024]{1,0:T(8,128)(2,1)} %bitcast.10, ...), custom_call_target="tpu_custom_call" | custom-call | tf_op jit(solution)/shard_map/conformer_conv/pallas_call | solution.py:571
  103.7 0.0 copy-start
  103.7 2.8 %copy.23 = bf16[1,768,1024]{2,1,0:T(8,128)(2,1)} copy(bf16[1,768,1024]{2,1,0:T(8,128)(2,1)} %bitcast.9) | data formatting | bytes 3145728
  106.5 0.0 copy-done
  106.5 0.0 copy-start.2
  106.5 0.0 copy-start.3
  106.5 0.0 copy-start.1
  106.5 0.0 copy-start.5
  106.5 0.0 copy-start.4
  106.6 1.1 %copy.24 = bf16[1,768,1024]{2,1,0:T(8,128)(2,1)} copy(bf16[1,768,1024]{2,1,0:T(8,128)(2,1)S(1)} %bitcast.8) | data formatting | bytes 3145728
  107.7 0.0 copy-done.2
  107.7 0.6 copy.25
  108.3 0.0 copy-done.3
  108.3 0.6 copy.26
  109.0 0.0 copy-done.1
  109.0 0.7 copy.27
  109.6 0.0 copy-done.5
  109.6 0.6 copy.28
  110.2 0.0 copy-done.4
  110.2 0.6 copy.29
Async XLA Ops:
  103.7 2.8 %copy-start = (bf16[768,1024]{1,0:T(8,128)(2,1)S(1)}, bf16[768,1024]{1,0:T(8,128)(2,1)}, u32[]{:S(2)}) copy-start(bf16[768,1024]{1,0:T(8,128)(2,1)} %get-tuple-element.15) | copy-start | bytes 4718596
  106.5 1.2 %copy-start.2 = (f32[8,2048]{1,0:T(8,128)S(1)}, f32[8,2048]{1,0:T(8,128)}, u32[]{:S(2)}) copy-start(f32[8,2048]{1,0:T(8,128)} %get-tuple-element.30) | copy-start | bytes 196612
  106.5 1.8 %copy-start.3 = (f32[8,1024]{1,0:T(8,128)S(1)}, f32[8,1024]{1,0:T(8,128)}, u32[]{:S(2)}) copy-start(f32[8,1024]{1,0:T(8,128)} %get-tuple-element.31) | copy-start | bytes 98308
  106.5 2.4 %copy-start.1 = (f32[31,1024]{1,0:T(8,128)S(1)}, f32[31,1024]{1,0:T(8,128)}, u32[]{:S(2)}) copy-start(f32[31,1024]{1,0:T(8,128)} %get-tuple-element.32) | copy-start | bytes 380932
  106.5 3.1 %copy-start.5 = (f32[8,128]{1,0:T(8,128)S(1)}, f32[8,128]{1,0:T(8,128)}, u32[]{:S(2)}) copy-start(f32[8,128]{1,0:T(8,128)} %get-tuple-element.19) | copy-start | bytes 12292
  106.5 3.7 %copy-start.4 = (f32[8,128]{1,0:T(8,128)S(1)}, f32[8,128]{1,0:T(8,128)}, u32[]{:S(2)}) copy-start(f32[8,128]{1,0:T(8,128)} %get-tuple-element.20) | copy-start | bytes 12292

commit v2 on v1

--- a/solution.py
+++ b/solution.py
@@ -19,10 +19,9 @@
 TAPS = 31
 COUNT = 58982.0
 NDP, NTM = 16, 8
-GRP = 8
+GRP = 12
 GROUPS = ROWS // (8 * GRP)
-MB = 256
-NB = 6
+NB = 5
 ORDERS = (("z", "x", "y"), ("x", "y", "z"), ("y", "z", "x"))
 
 
@@ -41,12 +40,13 @@
 def kernel(
     len_ref, frames_h, w_in_h, w_dw, gain_ref, bias_ref, w_out_h, cot_h,
     out_h, gf_h, gwi_ref, gwo_ref, gk_ref, gg_ref, gb_ref,
-    feats, w_in, w_out, cot, featsT, lin_v, sig_v, glu_p, dcv_p, conv_v, dsh_v,
+    feats, w_in, w_out, cot, featsT, stat_v, lin_v, sig_v, glu_p, dcv_p, conv_v, dsh_v,
     sw_v, swT, dpre_v, out_v, wb, vec,
     red, red_in, red_mid, red_rx1, red_rx2,
     gkl, kr1, ks1, kr2, kfull,
-    wl, crx, cs, r1, s1, r2, s2, r3,
-    in_sem, out_sem, halo_s, halo_r, ar1_s, ar1_r, ar2_s, ar2_r,
+    wl_a, crx_a, cs_a, r1_a, s1_a, r2_a, s2_a, r3_a,
+    wl_b, crx_b, cs_b, r1_b, s1_b, r2_b, s2_b, r3_b,
+    in_sem, w_sem, out_sem, halo_s, halo_r, ar1_s, ar1_r, ar2_s, ar2_r,
     k1_s, k1_r, k2_s, k2_r, k3_s, k3_r, rs_s, rs_r,
 ):
     dp = lax.axis_index("dp")
@@ -68,14 +68,21 @@
             device_id=dev, device_id_type=MESH_ID,
         )
 
+    def w_in_load(j, half):
+        cols = pl.ds(half * CH + j * 256, 256)
+        return pltpu.make_async_copy(w_in_h.at[:, cols], w_in.at[:, cols], w_sem.at[j, half])
+
     loads = [
         pltpu.make_async_copy(frames_h, feats, in_sem.at[0]),
-        pltpu.make_async_copy(w_in_h, w_in, in_sem.at[1]),
-        pltpu.make_async_copy(cot_h, cot, in_sem.at[2]),
-        pltpu.make_async_copy(w_out_h, w_out, in_sem.at[3]),
+        pltpu.make_async_copy(cot_h, cot, in_sem.at[1]),
+        pltpu.make_async_copy(w_out_h, w_out, in_sem.at[2]),
     ]
-    for c in loads:
-        c.start()
+    loads[0].start()
+    for j in range(4):
+        for half in range(2):
+            w_in_load(j, half).start()
+    loads[1].start()
+    loads[2].start()
     barrier = pltpu.get_barrier_semaphore()
     for d in range(1, NTM):
         pl.semaphore_signal(barrier, inc=1, device_id=(dp, (tm + d) % NTM), device_id_type=MESH_ID)
@@ -104,26 +111,21 @@
             ref[:, PAD + ROWS : PROWS, :] = jnp.zeros((CB, PAD, 128), F32)
 
     loads[0].wait()
-    loads[1].wait()
 
     @pl.loop(0, 4)
     def _(j):
         c0 = pl.multiple_of(j * 256, 256)
-
-        @pl.loop(0, ROWS // MB)
-        def _(m):
-            r0 = pl.multiple_of(m * MB, MB)
-            rows = feats[pl.ds(r0, MB), :]
-            lin = dot_nn(rows, w_in[:, pl.ds(c0, 256)])
-            sig = sigmoid(dot_nn(rows, w_in[:, pl.ds(CH + c0, 256)]))
-            glu = jnp.where(live_of(r0, MB, 256), lin * sig, 0.0).astype(BF16).astype(F32)
-            for h in range(2):
-                cols = slice(h * 128, h * 128 + 128)
-                lin_v[2 * j + h, pl.ds(r0, MB), :] = lin[:, cols]
-                sig_v[2 * j + h, pl.ds(r0, MB), :] = sig[:, cols]
-                glu_p[2 * j + h, pl.ds(PAD + r0, MB), :] = glu[:, cols]
-
-    pl.semaphore_wait(barrier, NTM + NDP - 2)
+        w_in_load(j, 0).wait()
+        w_in_load(j, 1).wait()
+        rows = feats[...]
+        lin = dot_nn(rows, w_in[:, pl.ds(c0, 256)])
+        sig = sigmoid(dot_nn(rows, w_in[:, pl.ds(CH + c0, 256)]))
+        glu = jnp.where(live_of(0, ROWS, 256), lin * sig, 0.0).astype(BF16).astype(F32)
+        for h in range(2):
+            cols = slice(h * 128, h * 128 + 128)
+            lin_v[2 * j + h] = lin[:, cols]
+            sig_v[2 * j + h] = sig[:, cols]
+            glu_p[2 * j + h, pl.ds(PAD, ROWS), :] = glu[:, cols]
 
     def halo(ref, n):
         to_left = rcopy(
@@ -150,53 +152,53 @@
         return start, recv, sent
 
     halo_g, halo_d = halo(glu_p, 0), halo(dcv_p, 2)
-    halo_g[0]()
-
-    loads[2].wait()
-    loads[3].wait()
-
-    @pl.loop(0, 4)
-    def _(j):
-        c0 = pl.multiple_of(j * 256, 256)
-
-        @pl.loop(0, ROWS // MB)
-        def _(m):
-            r0 = pl.multiple_of(m * MB, MB)
-            ds = dot_nt(cot[pl.ds(r0, MB), :], w_out[pl.ds(c0, 256), :])
-            for h in range(2):
-                dsh_v[2 * j + h, pl.ds(r0, MB), :] = ds[:, h * 128 : h * 128 + 128]
-
-    def taps_pass(src, cb, row0, tap_of):
-        acc = [None] * GRP
+    def taps_pass(src, cb, row0, tap_of, grp):
+        acc = [None] * grp
         for r in range(8):
-            xs = [src[cb, pl.ds(row0 + (8 * n + r), 8), :] for n in range(GRP + 3)]
+            xs = [src[cb, pl.ds(row0 + (8 * n + r), 8), :] for n in range(grp + 3)]
             for q in range(4):
                 o = 8 * q + r
                 if o == 0:
                     continue
                 w = wb[cb, tap_of(o)]
-                for g in range(GRP):
+                for g in range(grp):
                     term = w * xs[g + q]
                     acc[g] = term if acc[g] is None else acc[g] + term
         return acc
 
+    def conv_rows(cb, row0, grp, carry):
+        s, sq = carry
+        acc = taps_pass(glu_p, cb, row0, lambda o: o, grp)
+        for g in range(grp):
+            conv_v[cb, pl.ds(row0 + 8 * g, 8), :] = acc[g]
+            kept = jnp.where(live_of(row0 + 8 * g, 8, 128), acc[g], 0.0)
+            s = s + kept
+            sq = sq + kept * kept
+        return s, sq
+
+    EDGE, INNER = 8, 16
+
+    def conv_inner(cb):
+        def step(i, carry):
+            return conv_rows(cb, pl.multiple_of(64 + i * 128, 64), INNER, carry)
+
+        zero = jnp.zeros((8, 128), F32)
+        s, sq = lax.fori_loop(0, (ROWS - 128) // 128, step, (zero, zero))
+        stat_v[cb, 0] = s
+        stat_v[cb, 1] = sq
+
+    pl.loop(0, 2)(conv_inner)
+    pl.semaphore_wait(barrier, NTM + NDP - 2)
+    halo_g[0]()
+    pl.loop(2, CB)(conv_inner)
     halo_g[1]()
 
     @pl.loop(0, CB)
     def _(cb):
         def step(i, carry):
-            row0 = pl.multiple_of(i * (8 * GRP), 8 * GRP)
-            s, sq = carry
-            acc = taps_pass(glu_p, cb, row0, lambda o: o)
-            for g in range(GRP):
-                conv_v[cb, pl.ds(row0 + 8 * g, 8), :] = acc[g]
-                kept = jnp.where(live_of(row0 + 8 * g, 8, 128), acc[g], 0.0)
-                s = s + kept
-                sq = sq + kept * kept
-            return s, sq
-
-        zero = jnp.zeros((8, 128), F32)
-        s, sq = lax.fori_loop(0, GROUPS, step, (zero, zero))
+            return conv_rows(cb, pl.multiple_of(i * (ROWS - 64), 64), EDGE, carry)
+
+        s, sq = lax.fori_loop(0, 2, step, (stat_v[cb, 0], stat_v[cb, 1]))
         red[0, pl.ds(cb, 1), :] = jnp.sum(s, axis=0, keepdims=True)
         red[1, pl.ds(cb, 1), :] = jnp.sum(sq, axis=0, keepdims=True)
 
@@ -257,6 +259,16 @@
 
     ar_a, ar_b = all_sum(0), all_sum(1)
     ar_a[0]()
+
+    loads[1].wait()
+    loads[2].wait()
+
+    @pl.loop(0, 4)
+    def _(j):
+        c0 = pl.multiple_of(j * 256, 256)
+        ds = dot_nt(cot[...], w_out[pl.ds(c0, 256), :])
+        for h in range(2):
+            dsh_v[2 * j + h] = ds[:, h * 128 : h * 128 + 128]
 
     @pl.loop(0, 4)
     def _(i):
@@ -282,7 +294,7 @@
 
         def step(i, carry):
             sg, sb = carry
-            n = 64
+            n = 256
             row0 = pl.multiple_of(i * n, n)
             live = live_of(row0, n, 128)
             normed = (conv_v[cb, pl.ds(row0, n), :] - mean_r) * inv_r
@@ -300,35 +312,32 @@
             return sg, sb
 
         zero = jnp.zeros((8, 128), F32)
-        sg, sb = lax.fori_loop(0, ROWS // 64, step, (zero, zero))
+        sg, sb = lax.fori_loop(0, ROWS // 256, step, (zero, zero))
         red[0, pl.ds(cb, 1), :] = jnp.sum(sg, axis=0, keepdims=True)
         red[1, pl.ds(cb, 1), :] = jnp.sum(sb, axis=0, keepdims=True)
 
     ar_b[0]()
 
-    @pl.loop(0, ROWS // MB)
-    def _(m):
-        r0 = pl.multiple_of(m * MB, MB)
-        rows = jnp.concatenate([sw_v[cb, pl.ds(r0, MB), :] for cb in range(CB)], axis=1)
-
-        @pl.loop(0, 4)
-        def _(j):
-            c0 = pl.multiple_of(j * 256, 256)
-            out_v[0, pl.ds(r0, MB), pl.ds(c0, 256)] = dot_nn(rows, w_out[:, pl.ds(c0, 256)]).astype(BF16)
-
-    out_copy = pltpu.make_async_copy(out_v.at[0], out_h, out_sem.at[0])
-    out_copy.start()
-    ar_b[1]()
-
-    def put_terms(b, i, first, second):
+    def buf(name, b):
+        first, rest = rs_bufs[name]
+        return first if b == 0 else rest.at[b - 1]
+
+    rs_bufs = {
+        "wl": (wl_a, wl_b), "crx": (crx_a, crx_b), "cs": (cs_a, cs_b),
+        "r1": (r1_a, r1_b), "s1": (s1_a, s1_b), "r2": (r2_a, r2_b),
+        "s2": (s2_a, s2_b), "r3": (r3_a, r3_b),
+    }
+
+    def put_terms(dst, rows, cols, first, second):
+        n = first.shape[0] // 16
         both = jnp.concatenate(
-            [first.reshape(16, 2, 8, 256), second.reshape(16, 2, 8, 256)], axis=2
+            [first.reshape(n, 2, 8, 256), second.reshape(n, 2, 8, 256)], axis=2
         )
-        wl[b, pl.ds(16 * i, 16)] = both.astype(BF16)
+        dst[pl.ds(n * rows, n), :, :, cols] = both.astype(BF16)
 
     def rs_core(b):
         return rcopy(
-            wl.at[b, :, 1 - core], crx.at[b], rs_s.at[b, 0], rs_r.at[b, 0],
+            buf("wl", b).at[:, 1 - core], buf("crx", b), rs_s.at[b, 0], rs_r.at[b, 0],
             (dp, tm + 1 - 2 * core),
         )
 
@@ -339,7 +348,8 @@
     def rs_copies(b, stage):
         order = ORDERS[b % 3]
         dims = ("z", "x", "y")
-        src, dst = ((cs, r1), (s1, r2), (s2, r3))[stage]
+        src, dst = (("cs", "r1"), ("s1", "r2"), ("s2", "r3"))[stage]
+        src, dst = buf(src, b), buf(dst, b)
         dims = tuple(a for a in dims if a not in order[:stage])
         axis = order[stage]
         copies = []
@@ -347,12 +357,12 @@
             p = (pos[axis] + d) % 4
             copies.append(
                 rcopy(
-                    part_of(src.at[b], dims, axis, p), dst.at[b, d - 1],
+                    part_of(src, dims, axis, p), dst.at[d - 1],
                     rs_s.at[b, 3 * stage + d], rs_r.at[b, 3 * stage + d], at_axis(axis, p),
                 )
             )
-        own = part_of(src.at[b], dims, axis, pos[axis])
-        return copies, own, dst.at[b]
+        own = part_of(src, dims, axis, pos[axis])
+        return copies, own, dst
 
     def rs_one(b):
         rs_core(b).wait_recv()
@@ -360,8 +370,8 @@
         @pl.loop(0, 4)
         def _(i):
             rows = pl.ds(i * 16, 16)
-            both = wl[b, rows, core].astype(F32) + crx[b, rows].astype(F32)
-            cs[b, i] = both.astype(BF16).reshape(4, 4, 16, 256)
+            both = buf("wl", b)[rows, core].astype(F32) + buf("crx", b)[rows].astype(F32)
+            buf("cs", b)[i] = both.astype(BF16).reshape(4, 4, 16, both.shape[-1])
 
         for c in rs_copies(b, 0)[0]:
             c.start()
@@ -374,16 +384,16 @@
         for d in range(3):
             acc = acc + got[d].astype(F32)
         if stage < 2:
-            (s1, s2)[stage][b] = acc.astype(BF16)
+            buf(("s1", "s2")[stage], b)[...] = acc.astype(BF16)
             for c in rs_copies(b, stage + 1)[0]:
                 c.start()
         else:
             acc = acc * SCALE
-            if b < 2:
-                gwo_ref[:, 512 * b : 512 * b + 256] = acc[0:8]
-                gwo_ref[:, 512 * b + 256 : 512 * b + 512] = acc[8:16]
+            if b == 0:
+                gwo_ref[:, 0:512] = acc[0:8]
+                gwo_ref[:, 512:1024] = acc[8:16]
             else:
-                j = b - 2
+                j = b - 1
                 gwi_ref[:, 256 * j : 256 * j + 256] = acc[0:8]
                 gwi_ref[:, CH + 256 * j : CH + 256 * j + 256] = acc[8:16]
 
@@ -392,17 +402,30 @@
         for h in range(2):
             swT[pl.ds(256 * i + 128 * h, 128), :] = sw_v[2 * i + h].T
 
-    for b in range(2):
-        @pl.loop(0, 4)
+    for half in range(2):
+        cols = slice(256 * half, 256 * half + 256)
+
+        @pl.loop(0, 2)
         def _(i):
-            rows = swT[pl.ds(pl.multiple_of(256 * i, 256), 256), :]
+            rows = swT[pl.ds(pl.multiple_of(512 * i, 512), 512), :]
             put_terms(
-                b, i,
-                dot_nn(rows, cot[:, 512 * b : 512 * b + 256]),
-                dot_nn(rows, cot[:, 512 * b + 256 : 512 * b + 512]),
+                wl_a, i, cols,
+                dot_nn(rows, cot[:, 256 * half : 256 * half + 256]),
+                dot_nn(rows, cot[:, 512 + 256 * half : 512 + 256 * half + 256]),
             )
 
-        rs_core(b).start()
+    rs_core(0).start()
+    ar_b[1]()
+
+    @pl.loop(0, 4)
+    def _(j):
+        c0 = pl.multiple_of(j * 256, 256)
+        rows = jnp.concatenate([sw_v[cb] for cb in range(CB)], axis=1)
+        out_v[0, :, pl.ds(c0, 256)] = dot_nn(rows, w_out[:, pl.ds(c0, 256)]).astype(BF16)
+
+    out_copy = pltpu.make_async_copy(out_v.at[0], out_h, out_sem.at[0])
+    out_copy.start()
+    rs_one(0)
 
     grads = ar_b[2]()
     gg_ref[...] = grads[0] * SCALE
@@ -417,20 +440,17 @@
         shift = vec[5, pl.ds(cb, 1), :]
         tilt = vec[6, pl.ds(cb, 1), :]
 
-        @pl.loop(0, ROWS // 64)
+        @pl.loop(0, ROWS // 256)
         def _(i):
-            n = 64
+            n = 256
             row0 = pl.multiple_of(i * n, n)
             inner = dsh_v[cb, pl.ds(row0, n), :] - shift - conv_v[cb, pl.ds(row0, n), :] * tilt
             dcv = jnp.where(live_of(row0, n, 128), factor * inner, 0.0)
             dcv_p[cb, pl.ds(PAD + row0, n), :] = dcv.astype(BF16).astype(F32)
 
     halo_d[0]()
-    rs_one(0)
-    rs_one(1)
-
-    @pl.loop(0, CB)
-    def _(cb):
+
+    def kernel_grad(cb):
         def step(i, accs):
             row0 = pl.multiple_of(i * (8 * GRP), 8 * GRP)
             accs = list(accs)
@@ -451,23 +471,22 @@
             gkl[k, pl.ds(cb, 1), :] = jnp.sum(accs[k], axis=0, keepdims=True)
 
     gkl[TAPS] = jnp.zeros((8, 128), F32)
+    pl.loop(0, 5)(kernel_grad)
 
     kt1 = spread("tm", NTM, lambda p: gkl.at[pl.ds(4 * p, 4)], kr1, k1_s, k1_r)
     kt2 = spread("dp", NDP, lambda p: ks1.at[0], kr2, k2_s, k2_r)
     kt3 = spread("tm", NTM, lambda p: ks1.at[1], kfull, k3_s, k3_r)
-    kr1[tm] = gkl[pl.ds(4 * tm, 4)]
-    kt1[0]()
     halo_d[1]()
 
     def back_block(j):
-        b = 2 + j
+        b = 1 + j
         for h in range(2):
             cb = 2 * j + h
 
             @pl.loop(0, GROUPS)
             def _(i):
                 row0 = pl.multiple_of(i * (8 * GRP), 8 * GRP)
-                acc = taps_pass(dcv_p, cb, row0, lambda o: 32 - o)
+                acc = taps_pass(dcv_p, cb, row0, lambda o: 32 - o, GRP)
                 for g in range(0, GRP, 2):
                     dl, dg = [], []
                     for e in (g, g + 1):
@@ -484,68 +503,76 @@
         first = jnp.concatenate([dpre_v[2 * j], dpre_v[2 * j + 1]], axis=1)
         second = jnp.concatenate([dpre_v[CB + 2 * j], dpre_v[CB + 2 * j + 1]], axis=1)
 
-        @pl.loop(0, 4)
+        @pl.loop(0, 2)
         def _(i):
-            rows = featsT[pl.ds(pl.multiple_of(256 * i, 256), 256), :]
-            put_terms(b, i, dot_nn(rows, first), dot_nn(rows, second))
+            rows = featsT[pl.ds(pl.multiple_of(512 * i, 512), 512), :]
+            put_terms(buf("wl", b), i, slice(None), dot_nn(rows, first), dot_nn(rows, second))
 
         rs_core(b).start()
 
+    def kt_sum(n):
+        if n == 0:
+            kr1[tm] = gkl[pl.ds(4 * tm, 4)]
+            kt1[0]()
+        elif n == 1:
+            kt1[1]()
+            v = total(kr1, NTM)
+            ks1[0] = v
+            kr2[dp] = v
+            kt2[0]()
+        elif n == 2:
+            kt2[1]()
+            v = total(kr2, NDP)
+            ks1[1] = v
+            kfull[tm] = v
+            kt3[0]()
+        else:
+            kt3[1]()
+            for cb in range(CB):
+                for k in range(TAPS):
+                    row = kfull[k // 4, k % 4, cb : cb + 1, :]
+                    gk_ref[k : k + 1, 128 * cb : 128 * cb + 128] = row * SCALE
+
+    def frame_cols(j):
+        rows = jnp.concatenate([dpre_v[c] for c in range(2 * CB)], axis=1)
+        part = dot_nt(rows, w_in[256 * j : 256 * j + 256, :])
+        out_v[1, :, 256 * j : 256 * j + 256] = part.astype(BF16)
+
     back_block(0)
+    back_block(1)
+    rs_one(1)
     rs_next(0, 0)
-    rs_next(1, 0)
-    kt1[1]()
-    v = total(kr1, NTM)
-    ks1[0] = v
-    kr2[dp] = v
-    kt2[0]()
-    back_block(1)
+    back_block(2)
     rs_one(2)
     rs_next(0, 1)
+    back_block(3)
+    rs_one(3)
+    rs_next(1, 0)
+    pl.loop(5, CB)(kernel_grad)
+    kt_sum(0)
+    rs_one(4)
+    rs_next(0, 2)
+    rs_next(2, 0)
+
+    frame_cols(0)
     rs_next(1, 1)
-    kt2[1]()
-    v = total(kr2, NDP)
-    ks1[1] = v
-    kfull[tm] = v
-    kt3[0]()
-    back_block(2)
-    rs_one(3)
-    rs_next(2, 0)
-    rs_next(0, 2)
+    frame_cols(1)
+    rs_next(3, 0)
+    frame_cols(2)
+    kt_sum(1)
+    frame_cols(3)
+    gf_copy = pltpu.make_async_copy(out_v.at[1], gf_h, out_sem.at[1])
+    gf_copy.start()
+    rs_next(2, 1)
     rs_next(1, 2)
-    kt3[1]()
-    for cb in range(CB):
-        for k in range(TAPS):
-            gk_ref[k : k + 1, 128 * cb : 128 * cb + 128] = kfull[k // 4, k % 4, cb : cb + 1, :] * SCALE
-    back_block(3)
-    rs_one(4)
-    rs_next(3, 0)
-    rs_next(2, 1)
-
-    def frame_rows(m):
-        r0 = MB * m
-        rows = jnp.concatenate([dpre_v[c, pl.ds(r0, MB), :] for c in range(2 * CB)], axis=1)
-
-        @pl.loop(0, 4)
-        def _(j):
-            c0 = pl.multiple_of(j * 256, 256)
-            out_v[1, pl.ds(r0, MB), pl.ds(c0, 256)] = dot_nt(rows, w_in[pl.ds(c0, 256), :]).astype(BF16)
-
-    frame_rows(0)
-    rs_one(5)
     rs_next(4, 0)
     rs_next(3, 1)
+    kt_sum(2)
     rs_next(2, 2)
-    frame_rows(1)
-    rs_next(5, 0)
     rs_next(4, 1)
     rs_next(3, 2)
-    frame_rows(2)
-    gf_copy = pltpu.make_async_copy(out_v.at[1], gf_h, out_sem.at[1])
-    gf_copy.start()
-    rs_next(5, 1)
+    kt_sum(3)
     rs_next(4, 2)
-    rs_next(5, 2)
 
     for t in (halo_g, halo_d, kt1, kt2, kt3):
         t[2]()
@@ -561,6 +588,37 @@
 
 
 SCALE = 1.0 / math.sqrt(16 * 6144)
+
+
+def rs_scratch(lead, width):
+    shapes = (
+        (64, 2), (64,), (4, 4, 4), (3, 4, 4), (4, 4), (3, 4), (4,), (3,),
+    )
+    return [pltpu.VMEM((*lead, *s, 16, width), BF16) for s in shapes]
+
+
+PIECES = ((0, 4), (1, 4), (2, 1), (3, 1), (4, 1), (5, 1), (6, 1))
+
+
+def hand_over(*refs):
+    srcs, dsts, held, sems = refs[0:7], refs[7:14], refs[14:21], refs[21]
+    steps = []
+    for i, parts in PIECES:
+        rows = srcs[i].shape[0] // parts
+        for p in range(parts):
+            at = (pl.ds(p * rows, rows),)
+            n = len(steps)
+            steps.append((
+                pltpu.make_async_copy(srcs[i].at[at], held[i].at[at], sems.at[n, 0]),
+                pltpu.make_async_copy(held[i].at[at], dsts[i].at[at], sems.at[n, 1]),
+            ))
+    for come, _ in steps:
+        come.start()
+    for come, go in steps:
+        come.wait()
+        go.start()
+    for _, go in steps:
+        go.wait()
 
 
 def local(frames, lengths, w_in, w_dw, bn_gain, bn_bias, w_out, cotangent):
@@ -587,6 +645,7 @@
             pltpu.VMEM((CH, CH), BF16),
             pltpu.VMEM((ROWS, CH), BF16),
             pltpu.VMEM((CH, ROWS), BF16),
+            pltpu.VMEM((CB, 2, 8, 128), F32),
             pltpu.VMEM((CB, ROWS, 128), F32),
             pltpu.VMEM((CB, ROWS, 128), F32),
             pltpu.VMEM((CB, PROWS, 128), F32),
@@ -609,15 +668,10 @@
             pltpu.VMEM((2, 4, 8, 128), F32),
             pltpu.VMEM((NDP, 4, 8, 128), F32),
             pltpu.VMEM((NTM, 4, 8, 128), F32),
-            pltpu.VMEM((NB, 64, 2, 16, 256), BF16),
-            pltpu.VMEM((NB, 64, 16, 256), BF16),
-            pltpu.VMEM((NB, 4, 4, 4, 16, 256), BF16),
-            pltpu.VMEM((NB, 3, 4, 4, 16, 256), BF16),
-            pltpu.VMEM((NB, 4, 4, 16, 256), BF16),
-            pltpu.VMEM((NB, 3, 4, 16, 256), BF16),
-            pltpu.VMEM((NB, 4, 16, 256), BF16),
-            pltpu.VMEM((NB, 3, 16, 256), BF16),
-            dma((4,)),
+            *rs_scratch((), 512),
+            *rs_scratch((NB - 1,), 256),
+            dma((3,)),
+            dma((4, 2)),
             dma((2,)),
             dma((4,)),
             dma((4,)),
@@ -642,7 +696,14 @@
         lengths, frames[0], w_in, w_dw, bn_gain.reshape(8, 128), bn_bias.reshape(8, 128),
         w_out, cotangent[0],
     )
-    out, gf, gwi, gwo, gk, gg, gb = outs
+    out, gf, gwi, gwo, gk, gg, gb = pl.pallas_call(
+        hand_over,
+        out_shape=tuple(jax.ShapeDtypeStruct(o.shape, o.dtype) for o in outs),
+        in_specs=[hbm] * 7,
+        out_specs=(hbm,) * 7,
+        scratch_shapes=[pltpu.VMEM(o.shape, o.dtype) for o in outs] + [dma((13, 2))],
+        name="hand_over",
+    )(*outs)
     return (out[None], gf[None], gwi, gwo, gk, gg.reshape(CH), gb.reshape(CH))
 
 

time: 111 us -> 95.5 us (0.86)
  Pallas kernels: 102 us -> 93.1 us
  local copies, waits for them, and re-layouts: 7.04 us -> 0 us
    pallas_call x1, Pallas kernels: 102 us -> 90.1 us  [local(): pl.pallas_call(kernel, out_shape=(jax.ShapeDtypeStruct((ROWS, CH), BF16),...]
    unnamed x19 -> x0, local copies, waits for them, and re-layouts: 7.04 us -> none
    pallas_call x0 -> x1, Pallas kernels: none -> 2.95 us  [local(): pl.pallas_call(hand_over, out_shape=tuple((jax.ShapeDtypeStruct(o.shape,...]
where the time goes in v2:
time: 95.5 us; the launch traced here: 94.4 us
  Pallas kernels  93.1 us (97%)
  between operations  1.29 us (1%)
    pallas_call x1, Pallas kernels, local(): pl.pallas_call(kernel, out_shape=(jax.ShapeDtypeStruct((ROWS, CH), BF16),...  90.1 us
    pallas_call x1, Pallas kernels, local(): pl.pallas_call(hand_over, out_shape=tuple((jax.ShapeDtypeStruct(o.shape,...  2.95 us

profile of v2, /device:TPU:0, one launch (start us, length us, event | category | flops | bytes accessed | tf_op | source)
XLA Modules:
  0.0 94.4 jit_solution(7019622000616950428)
XLA Ops:
  1.3 90.1 %conformer_conv.1 = (bf16[768,1024]{1,0:T(8,128)(2,1)}, bf16[768,1024]{1,0:T(8,128)(2,1)}, f32[8,2048]{1,0:T(8,128)}, f32[8,1024]{1,0:T(8,128)}, f32[31,1024]{1,...) custom-call(s32[1]{0:T(128)S(6)} %copy.15.len_ref, bf16[768,1024]{1,0:T(8,128)(2,1)} %bitcast.8, ...), custom_call_target="tpu_custom_call" | custom-call | tf_op jit(solution)/shard_map/conformer_conv/pallas_call | solution.py:629
  91.4 3.0 %hand_over.1 = (bf16[768,1024]{1,0:T(8,128)(2,1)}, bf16[768,1024]{1,0:T(8,128)(2,1)}, f32[8,2048]{1,0:T(8,128)}, f32[8,1024]{1,0:T(8,128)}, f32[31,1024]{1,0:T(8...) custom-call(bf16[768,1024]{1,0:T(8,128)(2,1)} %get-tuple-element.21.refs_0_, bf16[768,1024]{1,0:T(8,128)(2,1)} %get-tuple-element.22.refs_1_, ...), custom_call_target="tpu_custom_call" | custom-call | tf_op jit(solution)/shard_map/hand_over/pallas_call | solution.py:699

commit v3 on v2

--- a/solution.py
+++ b/solution.py
@@ -21,7 +21,7 @@
 NDP, NTM = 16, 8
 GRP = 12
 GROUPS = ROWS // (8 * GRP)
-NB = 5
+NB = 6
 ORDERS = (("z", "x", "y"), ("x", "y", "z"), ("y", "z", "x"))
 
 
@@ -43,9 +43,10 @@
     feats, w_in, w_out, cot, featsT, stat_v, lin_v, sig_v, glu_p, dcv_p, conv_v, dsh_v,
     sw_v, swT, dpre_v, out_v, wb, vec,
     red, red_in, red_mid, red_rx1, red_rx2,
-    gkl, kr1, ks1, kr2, kfull,
+    gkl, gk1, gk2, gk3, kr1, ks1, kr2, kfull,
     wl_a, crx_a, cs_a, r1_a, s1_a, r2_a, s2_a, r3_a,
     wl_b, crx_b, cs_b, r1_b, s1_b, r2_b, s2_b, r3_b,
+    wl_c, crx_c, cs_c, r1_c, s1_c, r2_c, s2_c, r3_c,
     in_sem, w_sem, out_sem, halo_s, halo_r, ar1_s, ar1_r, ar2_s, ar2_r,
     k1_s, k1_r, k2_s, k2_r, k3_s, k3_r, rs_s, rs_r,
 ):
@@ -170,8 +171,8 @@
         s, sq = carry
         acc = taps_pass(glu_p, cb, row0, lambda o: o, grp)
         for g in range(grp):
-            conv_v[cb, pl.ds(row0 + 8 * g, 8), :] = acc[g]
             kept = jnp.where(live_of(row0 + 8 * g, 8, 128), acc[g], 0.0)
+            conv_v[cb, pl.ds(row0 + 8 * g, 8), :] = kept
             s = s + kept
             sq = sq + kept * kept
         return s, sq
@@ -179,11 +180,9 @@
     EDGE, INNER = 8, 16
 
     def conv_inner(cb):
-        def step(i, carry):
-            return conv_rows(cb, pl.multiple_of(64 + i * 128, 64), INNER, carry)
-
-        zero = jnp.zeros((8, 128), F32)
-        s, sq = lax.fori_loop(0, (ROWS - 128) // 128, step, (zero, zero))
+        s = sq = jnp.zeros((8, 128), F32)
+        for i in range((ROWS - 128) // 128):
+            s, sq = conv_rows(cb, 64 + i * 128, INNER, (s, sq))
         stat_v[cb, 0] = s
         stat_v[cb, 1] = sq
 
@@ -195,10 +194,9 @@
 
     @pl.loop(0, CB)
     def _(cb):
-        def step(i, carry):
-            return conv_rows(cb, pl.multiple_of(i * (ROWS - 64), 64), EDGE, carry)
-
-        s, sq = lax.fori_loop(0, 2, step, (stat_v[cb, 0], stat_v[cb, 1]))
+        s, sq = stat_v[cb, 0], stat_v[cb, 1]
+        for row0 in (0, ROWS - 64):
+            s, sq = conv_rows(cb, row0, EDGE, (s, sq))
         red[0, pl.ds(cb, 1), :] = jnp.sum(s, axis=0, keepdims=True)
         red[1, pl.ds(cb, 1), :] = jnp.sum(sq, axis=0, keepdims=True)
 
@@ -275,7 +273,54 @@
         c0 = pl.multiple_of(i * 256, 256)
         featsT[pl.ds(c0, 256), :] = feats[:, pl.ds(c0, 256)].T
 
+    def tap_sums(dst, grad):
+        grp = 16
+
+        @pl.loop(0, CB)
+        def _(cb):
+            def step(i, accs):
+                row0 = pl.multiple_of(i * (8 * grp), 8 * grp)
+                accs = list(accs)
+                ds = [grad[cb, pl.ds(row0 + 8 * g, 8), :] for g in range(grp)]
+                for r in range(8):
+                    xs = [glu_p[cb, pl.ds(row0 + (8 * n + r), 8), :] for n in range(grp + 3)]
+                    for q in range(4):
+                        o = 8 * q + r
+                        if o == 0:
+                            continue
+                        for g in range(grp):
+                            accs[o - 1] = accs[o - 1] + xs[g + q] * ds[g]
+                return tuple(accs)
+
+            zero = jnp.zeros((8, 128), F32)
+            accs = lax.fori_loop(0, ROWS // (8 * grp), step, (zero,) * TAPS)
+            for k in range(TAPS):
+                dst[k + 1, pl.ds(cb, 1), :] = jnp.sum(accs[k], axis=0, keepdims=True)
+
+    def window(rows_of):
+        count = jnp.clip(limit, 0, ROWS)
+        row, tap = rows_of
+        return ((row >= tap) & (row < count + tap)).astype(F32).astype(BF16)
+
+    def live_sums():
+        def grid(n):
+            return [lax.broadcasted_iota(jnp.int32, (32, n), d) for d in (1, 0)]
+
+        row, tap = grid(ROWS)
+        inner = window((row + PAD, tap))
+        row, tap = grid(2 * PAD)
+        outer = window((jnp.where(row < PAD, row, row + ROWS), tap))
+        for cb in range(CB):
+            ends = jnp.concatenate(
+                [glu_p[cb, 0:PAD, :], glu_p[cb, PAD + ROWS : PROWS, :]], axis=0
+            )
+            gk2[:, cb, :] = dot_nn(inner, glu_p[cb, PAD : PAD + ROWS, :].astype(BF16)) + dot_nn(
+                outer, ends.astype(BF16)
+            )
+
     ar_a[1]()
+    live_sums()
+    tap_sums(gk3, conv_v)
     sums = ar_a[2]()
     mean = sums[0] * (1.0 / COUNT)
     variance = sums[1] * (1.0 / COUNT) - mean * mean
@@ -319,20 +364,18 @@
     ar_b[0]()
 
     def buf(name, b):
-        first, rest = rs_bufs[name]
-        return first if b == 0 else rest.at[b - 1]
+        whole, pairs, singles = rs_bufs[name]
+        return whole if b == 0 else pairs.at[b - 1] if b < 4 else singles.at[b - 4]
 
     rs_bufs = {
-        "wl": (wl_a, wl_b), "crx": (crx_a, crx_b), "cs": (cs_a, cs_b),
-        "r1": (r1_a, r1_b), "s1": (s1_a, s1_b), "r2": (r2_a, r2_b),
-        "s2": (s2_a, s2_b), "r3": (r3_a, r3_b),
+        "wl": (wl_a, wl_b, wl_c), "crx": (crx_a, crx_b, crx_c), "cs": (cs_a, cs_b, cs_c),
+        "r1": (r1_a, r1_b, r1_c), "s1": (s1_a, s1_b, s1_c), "r2": (r2_a, r2_b, r2_c),
+        "s2": (s2_a, s2_b, s2_c), "r3": (r3_a, r3_b, r3_c),
     }
 
     def put_terms(dst, rows, cols, first, second):
-        n = first.shape[0] // 16
-        both = jnp.concatenate(
-            [first.reshape(n, 2, 8, 256), second.reshape(n, 2, 8, 256)], axis=2
-        )
+        n, w = first.shape[0] // 16, first.shape[1]
+        both = jnp.concatenate([first.reshape(n, 2, 8, w), second.reshape(n, 2, 8, w)], axis=2)
         dst[pl.ds(n * rows, n), :, :, cols] = both.astype(BF16)
 
     def rs_core(b):
@@ -393,9 +436,9 @@
                 gwo_ref[:, 0:512] = acc[0:8]
                 gwo_ref[:, 512:1024] = acc[8:16]
             else:
-                j = b - 1
-                gwi_ref[:, 256 * j : 256 * j + 256] = acc[0:8]
-                gwi_ref[:, CH + 256 * j : CH + 256 * j + 256] = acc[8:16]
+                c0, w = (256 * (b - 1), 256) if b < 4 else (128 * (b + 2), 128)
+                gwi_ref[:, c0 : c0 + w] = acc[0:8]
+                gwi_ref[:, CH + c0 : CH + c0 + w] = acc[8:16]
 
     @pl.loop(0, 4)
     def _(i):
@@ -417,14 +460,7 @@
     rs_core(0).start()
     ar_b[1]()
 
-    @pl.loop(0, 4)
-    def _(j):
-        c0 = pl.multiple_of(j * 256, 256)
-        rows = jnp.concatenate([sw_v[cb] for cb in range(CB)], axis=1)
-        out_v[0, :, pl.ds(c0, 256)] = dot_nn(rows, w_out[:, pl.ds(c0, 256)]).astype(BF16)
-
-    out_copy = pltpu.make_async_copy(out_v.at[0], out_h, out_sem.at[0])
-    out_copy.start()
+    tap_sums(gk1, dsh_v)
     rs_one(0)
 
     grads = ar_b[2]()
@@ -434,79 +470,77 @@
     vec[5] = grads[1] * (1.0 / COUNT)
     vec[6] = grads[0] * (1.0 / COUNT)
 
-    @pl.loop(0, CB)
-    def _(cb):
-        factor = vec[4, pl.ds(cb, 1), :]
-        shift = vec[5, pl.ds(cb, 1), :]
-        tilt = vec[6, pl.ds(cb, 1), :]
-
-        @pl.loop(0, ROWS // 256)
-        def _(i):
-            n = 256
-            row0 = pl.multiple_of(i * n, n)
-            inner = dsh_v[cb, pl.ds(row0, n), :] - shift - conv_v[cb, pl.ds(row0, n), :] * tilt
-            dcv = jnp.where(live_of(row0, n, 128), factor * inner, 0.0)
-            dcv_p[cb, pl.ds(PAD + row0, n), :] = dcv.astype(BF16).astype(F32)
-
+    def dconv_rows(parts):
+        @pl.loop(0, CB)
+        def _(cb):
+            factor = vec[4, pl.ds(cb, 1), :]
+            shift = vec[5, pl.ds(cb, 1), :]
+            tilt = vec[6, pl.ds(cb, 1), :]
+            for row0, n in parts:
+                rows = pl.ds(row0, n)
+                inner = dsh_v[cb, rows, :] - shift - conv_v[cb, rows, :] * tilt
+                dcv = jnp.where(live_of(row0, n, 128), factor * inner, 0.0)
+                dcv_p[cb, pl.ds(PAD + row0, n), :] = dcv.astype(BF16).astype(F32)
+
+    dconv_rows(((0, PAD), (ROWS - PAD, PAD)))
     halo_d[0]()
 
-    def kernel_grad(cb):
-        def step(i, accs):
-            row0 = pl.multiple_of(i * (8 * GRP), 8 * GRP)
-            accs = list(accs)
-            ds = [dcv_p[cb, pl.ds(row0 + PAD + 8 * g, 8), :] for g in range(GRP)]
-            for r in range(8):
-                xs = [glu_p[cb, pl.ds(row0 + (8 * n + r), 8), :] for n in range(GRP + 3)]
-                for q in range(4):
-                    o = 8 * q + r
-                    if o == 0:
-                        continue
-                    for g in range(GRP):
-                        accs[o - 1] = accs[o - 1] + xs[g + q] * ds[g]
-            return tuple(accs)
-
-        zero = jnp.zeros((8, 128), F32)
-        accs = lax.fori_loop(0, GROUPS, step, (zero,) * TAPS)
-        for k in range(TAPS):
-            gkl[k, pl.ds(cb, 1), :] = jnp.sum(accs[k], axis=0, keepdims=True)
-
+    mean, inv_std = vec[0], vec[1]
+    for o in range(1, TAPS + 1):
+        tilted = inv_std * (gk3[o] - mean * gk2[o])
+        gkl[o - 1] = vec[4] * (gk1[o] - vec[5] * gk2[o] - vec[6] * tilted)
     gkl[TAPS] = jnp.zeros((8, 128), F32)
-    pl.loop(0, 5)(kernel_grad)
 
     kt1 = spread("tm", NTM, lambda p: gkl.at[pl.ds(4 * p, 4)], kr1, k1_s, k1_r)
     kt2 = spread("dp", NDP, lambda p: ks1.at[0], kr2, k2_s, k2_r)
     kt3 = spread("tm", NTM, lambda p: ks1.at[1], kfull, k3_s, k3_r)
-    halo_d[1]()
-
-    def back_block(j):
-        b = 1 + j
-        for h in range(2):
-            cb = 2 * j + h
-
-            @pl.loop(0, GROUPS)
-            def _(i):
-                row0 = pl.multiple_of(i * (8 * GRP), 8 * GRP)
-                acc = taps_pass(dcv_p, cb, row0, lambda o: 32 - o, GRP)
-                for g in range(0, GRP, 2):
-                    dl, dg = [], []
-                    for e in (g, g + 1):
-                        rows = pl.ds(row0 + 8 * e, 8)
-                        dglu = jnp.where(live_of(row0 + 8 * e, 8, 128), acc[e], 0.0)
-                        sig = sig_v[cb, rows, :]
-                        half = dglu * sig
-                        dl.append(half)
-                        dg.append(half * lin_v[cb, rows, :] * (1.0 - sig))
-                    rows = pl.ds(row0 + 8 * g, 16)
-                    dpre_v[cb, rows, :] = jnp.concatenate(dl, axis=0).astype(BF16)
-                    dpre_v[CB + cb, rows, :] = jnp.concatenate(dg, axis=0).astype(BF16)
-
+    def back_rows(cb, row0, grp):
+        acc = taps_pass(dcv_p, cb, row0, lambda o: 32 - o, grp)
+        for g in range(0, grp, 2):
+            dl, dg = [], []
+            for e in (g, g + 1):
+                rows = pl.ds(row0 + 8 * e, 8)
+                dglu = jnp.where(live_of(row0 + 8 * e, 8, 128), acc[e], 0.0)
+                sig = sig_v[cb, rows, :]
+                half = dglu * sig
+                dl.append(half)
+                dg.append(half * lin_v[cb, rows, :] * (1.0 - sig))
+            rows = pl.ds(row0 + 8 * g, 16)
+            dpre_v[cb, rows, :] = jnp.concatenate(dl, axis=0).astype(BF16)
+            dpre_v[CB + cb, rows, :] = jnp.concatenate(dg, axis=0).astype(BF16)
+
+    def back_inner(cb):
+        for i in range((ROWS - 128) // 128):
+            back_rows(cb, 64 + 128 * i, INNER)
+
+    def back_edges(cb):
+        for row0 in (0, ROWS - 64):
+            back_rows(cb, row0, EDGE)
+
+    def back_all(cb):
+        for i in range(GROUPS):
+            back_rows(cb, 8 * GRP * i, GRP)
+
+    def pair_terms(j):
         first = jnp.concatenate([dpre_v[2 * j], dpre_v[2 * j + 1]], axis=1)
         second = jnp.concatenate([dpre_v[CB + 2 * j], dpre_v[CB + 2 * j + 1]], axis=1)
 
         @pl.loop(0, 2)
         def _(i):
             rows = featsT[pl.ds(pl.multiple_of(512 * i, 512), 512), :]
-            put_terms(buf("wl", b), i, slice(None), dot_nn(rows, first), dot_nn(rows, second))
+            put_terms(buf("wl", 1 + j), i, slice(None), dot_nn(rows, first), dot_nn(rows, second))
+
+        rs_core(1 + j).start()
+
+    def single_terms(b):
+        cb = b + 2
+        both = jnp.concatenate([dpre_v[cb], dpre_v[CB + cb]], axis=1)
+
+        @pl.loop(0, 2)
+        def _(i):
+            rows = featsT[pl.ds(pl.multiple_of(512 * i, 512), 512), :]
+            part = dot_nn(rows, both)
+            put_terms(buf("wl", b), i, slice(None), part[:, 0:128], part[:, 128:256])
 
         rs_core(b).start()
 
@@ -538,41 +572,64 @@
         part = dot_nt(rows, w_in[256 * j : 256 * j + 256, :])
         out_v[1, :, 256 * j : 256 * j + 256] = part.astype(BF16)
 
-    back_block(0)
-    back_block(1)
+    def out_cols(j):
+        rows = jnp.concatenate([sw_v[cb] for cb in range(CB)], axis=1)
+        part = dot_nn(rows, w_out[:, 256 * j : 256 * j + 256])
+        out_v[0, :, 256 * j : 256 * j + 256] = part.astype(BF16)
+
+    kt_sum(0)
+    dconv_rows(((PAD, 384), (PAD + 384, 352)))
+    pl.loop(0, 2)(back_inner)
+    halo_d[1]()
+    pl.loop(0, 2)(back_edges)
+    pair_terms(0)
+    kt_sum(1)
+    pl.loop(2, 4)(back_all)
+    pair_terms(1)
     rs_one(1)
+    pl.loop(4, 6)(back_all)
+    pair_terms(2)
+    rs_one(2)
+    kt_sum(2)
     rs_next(0, 0)
-    back_block(2)
-    rs_one(2)
+    pl.loop(6, 7)(back_all)
+    single_terms(4)
+    rs_one(3)
+    pl.loop(7, 8)(back_all)
+    single_terms(5)
+    rs_one(4)
+
+    frame_cols(0)
+    rs_one(5)
+    rs_next(1, 0)
+    frame_cols(1)
     rs_next(0, 1)
-    back_block(3)
-    rs_one(3)
-    rs_next(1, 0)
-    pl.loop(5, CB)(kernel_grad)
-    kt_sum(0)
-    rs_one(4)
-    rs_next(0, 2)
     rs_next(2, 0)
-
-    frame_cols(0)
-    rs_next(1, 1)
-    frame_cols(1)
+    frame_cols(2)
     rs_next(3, 0)
-    frame_cols(2)
-    kt_sum(1)
     frame_cols(3)
     gf_copy = pltpu.make_async_copy(out_v.at[1], gf_h, out_sem.at[1])
     gf_copy.start()
+    rs_next(4, 0)
+    rs_next(1, 1)
+    out_cols(0)
+    out_cols(1)
+    rs_next(5, 0)
     rs_next(2, 1)
+    out_cols(2)
+    out_cols(3)
+    out_copy = pltpu.make_async_copy(out_v.at[0], out_h, out_sem.at[0])
+    out_copy.start()
+    rs_next(3, 1)
+    rs_next(4, 1)
+    rs_next(0, 2)
+    kt_sum(3)
+    rs_next(5, 1)
     rs_next(1, 2)
-    rs_next(4, 0)
-    rs_next(3, 1)
-    kt_sum(2)
     rs_next(2, 2)
-    rs_next(4, 1)
     rs_next(3, 2)
-    kt_sum(3)
     rs_next(4, 2)
+    rs_next(5, 2)
 
     for t in (halo_g, halo_d, kt1, kt2, kt3):
         t[2]()
@@ -664,12 +721,16 @@
             pltpu.VMEM((2, NTM, 2, 8, 128), F32),
             pltpu.VMEM((2, NDP, 2, 8, 128), F32),
             pltpu.VMEM((32, 8, 128), F32),
+            pltpu.VMEM((32, 8, 128), F32),
+            pltpu.VMEM((32, 8, 128), F32),
+            pltpu.VMEM((32, 8, 128), F32),
             pltpu.VMEM((NTM, 4, 8, 128), F32),
             pltpu.VMEM((2, 4, 8, 128), F32),
             pltpu.VMEM((NDP, 4, 8, 128), F32),
             pltpu.VMEM((NTM, 4, 8, 128), F32),
             *rs_scratch((), 512),
-            *rs_scratch((NB - 1,), 256),
+            *rs_scratch((3,), 256),
+            *rs_scratch((2,), 128),
             dma((3,)),
             dma((4, 2)),
             dma((2,)),

time: 95.5 us -> 90.4 us (0.947); the launches traced: 94.4 us -> 90.3 us
  Pallas kernels: 93.1 us -> 88.8 us
    pallas_call x1, Pallas kernels: 90.1 us -> 85.9 us  [local(): pl.pallas_call(kernel, out_shape=(jax.ShapeDtypeStruct((ROWS, CH), BF16),...]
where the time goes in v3:
time: 90.4 us; the launch traced here: 90.3 us
  Pallas kernels  88.8 us (98%)
  between operations  1.45 us (2%)
    pallas_call x1, Pallas kernels, local(): pl.pallas_call(kernel, out_shape=(jax.ShapeDtypeStruct((ROWS, CH), BF16),...  85.9 us
    pallas_call x1, Pallas kernels, local(): pl.pallas_call(hand_over, out_shape=tuple((jax.ShapeDtypeStruct(o.shape,...  2.95 us

profile of v3, /device:TPU:0, one launch (start us, length us, event | category | flops | bytes accessed | tf_op | source)
XLA Modules:
  0.0 90.3 jit_solution(8301782451472785629)
XLA Ops:
  1.3 85.9 %conformer_conv.1 = (bf16[768,1024]{1,0:T(8,128)(2,1)}, bf16[768,1024]{1,0:T(8,128)(2,1)}, f32[8,2048]{1,0:T(8,128)}, f32[8,1024]{1,0:T(8,128)}, f32[31,1024]{1,...) custom-call(s32[1]{0:T(128)S(6)} %copy.15.len_ref, bf16[768,1024]{1,0:T(8,128)(2,1)} %bitcast.8, ...), custom_call_target="tpu_custom_call" | custom-call | tf_op jit(solution)/shard_map/conformer_conv/pallas_call | solution.py:686
  87.2 3.0 %hand_over.1 = (bf16[768,1024]{1,0:T(8,128)(2,1)}, bf16[768,1024]{1,0:T(8,128)(2,1)}, f32[8,2048]{1,0:T(8,128)}, f32[8,1024]{1,0:T(8,128)}, f32[31,1024]{1,0:T(8...) custom-call(bf16[768,1024]{1,0:T(8,128)(2,1)} %get-tuple-element.21.refs_0_, bf16[768,1024]{1,0:T(8,128)(2,1)} %get-tuple-element.22.refs_1_, ...), custom_call_target="tpu_custom_call" | custom-call | tf_op jit(solution)/shard_map/hand_over/pallas_call | solution.py:760

commit v4 on v3

--- a/solution.py
+++ b/solution.py
@@ -22,7 +22,7 @@
 GRP = 12
 GROUPS = ROWS // (8 * GRP)
 NB = 6
-ORDERS = (("z", "x", "y"), ("x", "y", "z"), ("y", "z", "x"))
+ORDER = ("z", "x", "y")
 
 
 def sigmoid(x):
@@ -31,6 +31,10 @@
 
 def dot_nn(a, b):
     return lax.dot_general(a, b, (((1,), (0,)), ((), ())), preferred_element_type=F32)
+
+
+def dot_tn(a, b):
+    return lax.dot_general(a, b, (((0,), (0,)), ((), ())), preferred_element_type=F32)
 
 
 def dot_nt(a, b):
@@ -40,10 +44,10 @@
 def kernel(
     len_ref, frames_h, w_in_h, w_dw, gain_ref, bias_ref, w_out_h, cot_h,
     out_h, gf_h, gwi_ref, gwo_ref, gk_ref, gg_ref, gb_ref,
-    feats, w_in, w_out, cot, featsT, stat_v, lin_v, sig_v, glu_p, dcv_p, conv_v, dsh_v,
-    sw_v, swT, dpre_v, out_v, wb, vec,
+    feats, w_in, w_out, cot, stat_v, lin_v, sig_v, glu_p, dcv_p, conv_v, dsh_v,
+    sw_v, dpre_v, out_v, wb, vec,
     red, red_in, red_mid, red_rx1, red_rx2,
-    gkl, gk1, gk2, gk3, kr1, ks1, kr2, kfull,
+    gkl, gk1, gk2, gk3, kr1, ks1, kr2, ks2, kfull,
     wl_a, crx_a, cs_a, r1_a, s1_a, r2_a, s2_a, r3_a,
     wl_b, crx_b, cs_b, r1_b, s1_b, r2_b, s2_b, r3_b,
     wl_c, crx_c, cs_c, r1_c, s1_c, r2_c, s2_c, r3_c,
@@ -223,9 +227,9 @@
         return start, recv, sent
 
     def total(ref, count):
-        acc = ref[0]
+        acc = ref[0].astype(F32)
         for i in range(1, count):
-            acc = acc + ref[i]
+            acc = acc + ref[i].astype(F32)
         return acc
 
     def all_sum(n):
@@ -268,16 +272,13 @@
         for h in range(2):
             dsh_v[2 * j + h] = ds[:, h * 128 : h * 128 + 128]
 
-    @pl.loop(0, 4)
-    def _(i):
-        c0 = pl.multiple_of(i * 256, 256)
-        featsT[pl.ds(c0, 256), :] = feats[:, pl.ds(c0, 256)].T
-
-    def tap_sums(dst, grad):
+    def tap_sums(dst, grad, first_blocks, between):
         grp = 16
 
         @pl.loop(0, CB)
         def _(cb):
+            pl.when(cb == first_blocks)(between)
+
             def step(i, accs):
                 row0 = pl.multiple_of(i * (8 * grp), 8 * grp)
                 accs = list(accs)
@@ -318,9 +319,7 @@
                 outer, ends.astype(BF16)
             )
 
-    ar_a[1]()
-    live_sums()
-    tap_sums(gk3, conv_v)
+    tap_sums(gk3, conv_v, 1, ar_a[1])
     sums = ar_a[2]()
     mean = sums[0] * (1.0 / COUNT)
     variance = sums[1] * (1.0 / COUNT) - mean * mean
@@ -389,13 +388,26 @@
         return ref.at[tuple(slice(None) for _ in range(at)) + (p,)]
 
     def rs_copies(b, stage):
-        order = ORDERS[b % 3]
         dims = ("z", "x", "y")
-        src, dst = (("cs", "r1"), ("s1", "r2"), ("s2", "r3"))[stage]
+        if b == 0:
+            src, dst = (("cs", "r1"), ("s1", "r2"), ("s2", "r3"))[stage]
+            dims = tuple(a for a in dims if a not in ORDER[:stage])
+            axis = ORDER[stage]
+        else:
+            src, dst = (("cs", "r1"), ("s1", "r2"))[stage]
+            axis = ("y", "dp")[stage]
         src, dst = buf(src, b), buf(dst, b)
-        dims = tuple(a for a in dims if a not in order[:stage])
-        axis = order[stage]
         copies = []
+        if axis == "dp":
+            for d in range(1, NDP):
+                p = (dp + d) % NDP
+                copies.append(
+                    rcopy(
+                        src.at[p // 4, p % 4], dst.at[d - 1],
+                        rs_s.at[b, 3 + d], rs_r.at[b, 3 + d], (p, tm),
+                    )
+                )
+            return copies, src.at[z, x], dst
         for d in range(1, 4):
             p = (pos[axis] + d) % 4
             copies.append(
@@ -404,8 +416,10 @@
                     rs_s.at[b, 3 * stage + d], rs_r.at[b, 3 * stage + d], at_axis(axis, p),
                 )
             )
-        own = part_of(src, dims, axis, pos[axis])
-        return copies, own, dst
+        return copies, part_of(src, dims, axis, pos[axis]), dst
+
+    def stages(b):
+        return 3 if b == 0 else 2
 
     def rs_one(b):
         rs_core(b).wait_recv()
@@ -424,9 +438,9 @@
         for c in copies:
             c.wait_recv()
         acc = own[...].astype(F32)
-        for d in range(3):
+        for d in range(len(copies)):
             acc = acc + got[d].astype(F32)
-        if stage < 2:
+        if stage < stages(b) - 1:
             buf(("s1", "s2")[stage], b)[...] = acc.astype(BF16)
             for c in rs_copies(b, stage + 1)[0]:
                 c.start()
@@ -440,27 +454,19 @@
                 gwi_ref[:, c0 : c0 + w] = acc[0:8]
                 gwi_ref[:, CH + c0 : CH + c0 + w] = acc[8:16]
 
-    @pl.loop(0, 4)
-    def _(i):
-        for h in range(2):
-            swT[pl.ds(256 * i + 128 * h, 128), :] = sw_v[2 * i + h].T
-
     for half in range(2):
         cols = slice(256 * half, 256 * half + 256)
-
-        @pl.loop(0, 2)
-        def _(i):
-            rows = swT[pl.ds(pl.multiple_of(512 * i, 512), 512), :]
+        for i in range(2):
+            rows = jnp.concatenate([sw_v[4 * i + e] for e in range(4)], axis=1)
             put_terms(
                 wl_a, i, cols,
-                dot_nn(rows, cot[:, 256 * half : 256 * half + 256]),
-                dot_nn(rows, cot[:, 512 + 256 * half : 512 + 256 * half + 256]),
+                dot_tn(rows, cot[:, 256 * half : 256 * half + 256]),
+                dot_tn(rows, cot[:, 512 + 256 * half : 512 + 256 * half + 256]),
             )
 
     rs_core(0).start()
-    ar_b[1]()
-
-    tap_sums(gk1, dsh_v)
+    tap_sums(gk1, dsh_v, 2, ar_b[1])
+    live_sums()
     rs_one(0)
 
     grads = ar_b[2]()
@@ -486,14 +492,19 @@
     halo_d[0]()
 
     mean, inv_std = vec[0], vec[1]
-    for o in range(1, TAPS + 1):
-        tilted = inv_std * (gk3[o] - mean * gk2[o])
-        gkl[o - 1] = vec[4] * (gk1[o] - vec[5] * gk2[o] - vec[6] * tilted)
-    gkl[TAPS] = jnp.zeros((8, 128), F32)
-
-    kt1 = spread("tm", NTM, lambda p: gkl.at[pl.ds(4 * p, 4)], kr1, k1_s, k1_r)
-    kt2 = spread("dp", NDP, lambda p: ks1.at[0], kr2, k2_s, k2_r)
-    kt3 = spread("tm", NTM, lambda p: ks1.at[1], kfull, k3_s, k3_r)
+
+    def tap_row(k):
+        if k == TAPS:
+            return jnp.zeros((8, 128), F32)
+        tilted = inv_std * (gk3[k + 1] - mean * gk2[k + 1])
+        return vec[4] * (gk1[k + 1] - vec[5] * gk2[k + 1] - vec[6] * tilted)
+
+    for k in range(0, 32, 2):
+        gkl[k // 2] = jnp.concatenate([tap_row(k), tap_row(k + 1)], axis=0).astype(BF16)
+
+    kt1 = spread("tm", NTM, lambda p: gkl.at[pl.ds(2 * p, 2)], kr1, k1_s, k1_r)
+    kt2 = spread("dp", NDP, lambda p: ks1, kr2, k2_s, k2_r)
+    kt3 = spread("tm", NTM, lambda p: ks2, kfull, k3_s, k3_r)
     def back_rows(cb, row0, grp):
         acc = taps_pass(dcv_p, cb, row0, lambda o: 32 - o, grp)
         for g in range(0, grp, 2):
@@ -527,8 +538,8 @@
 
         @pl.loop(0, 2)
         def _(i):
-            rows = featsT[pl.ds(pl.multiple_of(512 * i, 512), 512), :]
-            put_terms(buf("wl", 1 + j), i, slice(None), dot_nn(rows, first), dot_nn(rows, second))
+            rows = feats[:, pl.ds(pl.multiple_of(512 * i, 512), 512)]
+            put_terms(buf("wl", 1 + j), i, slice(None), dot_tn(rows, first), dot_tn(rows, second))
 
         rs_core(1 + j).start()
 
@@ -538,33 +549,34 @@
 
         @pl.loop(0, 2)
         def _(i):
-            rows = featsT[pl.ds(pl.multiple_of(512 * i, 512), 512), :]
-            part = dot_nn(rows, both)
+            rows = feats[:, pl.ds(pl.multiple_of(512 * i, 512), 512)]
+            part = dot_tn(rows, both)
             put_terms(buf("wl", b), i, slice(None), part[:, 0:128], part[:, 128:256])
 
         rs_core(b).start()
 
     def kt_sum(n):
         if n == 0:
-            kr1[tm] = gkl[pl.ds(4 * tm, 4)]
+            kr1[tm] = gkl[pl.ds(2 * tm, 2)]
             kt1[0]()
         elif n == 1:
             kt1[1]()
-            v = total(kr1, NTM)
-            ks1[0] = v
+            v = total(kr1, NTM).astype(BF16)
+            ks1[...] = v
             kr2[dp] = v
             kt2[0]()
         elif n == 2:
             kt2[1]()
             v = total(kr2, NDP)
-            ks1[1] = v
+            ks2[...] = v
             kfull[tm] = v
             kt3[0]()
         else:
             kt3[1]()
             for cb in range(CB):
                 for k in range(TAPS):
-                    row = kfull[k // 4, k % 4, cb : cb + 1, :]
+                    at = 8 * (k % 2) + cb
+                    row = kfull[k // 4, k % 4 // 2, at : at + 1, :]
                     gk_ref[k : k + 1, 128 * cb : 128 * cb + 128] = row * SCALE
 
     def frame_cols(j):
@@ -603,33 +615,28 @@
     rs_one(5)
     rs_next(1, 0)
     frame_cols(1)
+    frame_cols(2)
     rs_next(0, 1)
-    rs_next(2, 0)
-    frame_cols(2)
-    rs_next(3, 0)
     frame_cols(3)
     gf_copy = pltpu.make_async_copy(out_v.at[1], gf_h, out_sem.at[1])
     gf_copy.start()
-    rs_next(4, 0)
-    rs_next(1, 1)
+    rs_next(2, 0)
     out_cols(0)
     out_cols(1)
-    rs_next(5, 0)
-    rs_next(2, 1)
+    rs_next(3, 0)
     out_cols(2)
     out_cols(3)
     out_copy = pltpu.make_async_copy(out_v.at[0], out_h, out_sem.at[0])
     out_copy.start()
+    rs_next(4, 0)
+    rs_next(5, 0)
+    kt_sum(3)
+    rs_next(0, 2)
+    rs_next(1, 1)
+    rs_next(2, 1)
     rs_next(3, 1)
     rs_next(4, 1)
-    rs_next(0, 2)
-    kt_sum(3)
     rs_next(5, 1)
-    rs_next(1, 2)
-    rs_next(2, 2)
-    rs_next(3, 2)
-    rs_next(4, 2)
-    rs_next(5, 2)
 
     for t in (halo_g, halo_d, kt1, kt2, kt3):
         t[2]()
@@ -637,7 +644,7 @@
     ar_b[3]()
     for b in range(NB):
         rs_core(b).wait_send()
-        for stage in range(3):
+        for stage in range(stages(b)):
             for c in rs_copies(b, stage)[0]:
                 c.wait_send()
     out_copy.wait()
@@ -648,9 +655,9 @@
 
 
 def rs_scratch(lead, width):
-    shapes = (
-        (64, 2), (64,), (4, 4, 4), (3, 4, 4), (4, 4), (3, 4), (4,), (3,),
-    )
+    shapes = [(64, 2), (64,), (4, 4, 4), (3, 4, 4), (4, 4), (3, 4), (4,), (3,)]
+    if lead:
+        shapes[5:] = [(15,), (1,), (1,)]
     return [pltpu.VMEM((*lead, *s, 16, width), BF16) for s in shapes]
 
 
@@ -701,7 +708,6 @@
             pltpu.VMEM((CH, 2 * CH), BF16),
             pltpu.VMEM((CH, CH), BF16),
             pltpu.VMEM((ROWS, CH), BF16),
-            pltpu.VMEM((CH, ROWS), BF16),
             pltpu.VMEM((CB, 2, 8, 128), F32),
             pltpu.VMEM((CB, ROWS, 128), F32),
             pltpu.VMEM((CB, ROWS, 128), F32),
@@ -710,7 +716,6 @@
             pltpu.VMEM((CB, ROWS, 128), F32),
             pltpu.VMEM((CB, ROWS, 128), F32),
             pltpu.VMEM((CB, ROWS, 128), BF16),
-            pltpu.VMEM((CH, ROWS), BF16),
             pltpu.VMEM((2 * CB, ROWS, 128), BF16),
             pltpu.VMEM((2, ROWS, CH), BF16),
             pltpu.VMEM((CB, 32, 8, 128), F32),
@@ -720,14 +725,15 @@
             pltpu.VMEM((2, 2, 8, 128), F32),
             pltpu.VMEM((2, NTM, 2, 8, 128), F32),
             pltpu.VMEM((2, NDP, 2, 8, 128), F32),
+            pltpu.VMEM((16, 16, 128), BF16),
             pltpu.VMEM((32, 8, 128), F32),
             pltpu.VMEM((32, 8, 128), F32),
             pltpu.VMEM((32, 8, 128), F32),
-            pltpu.VMEM((32, 8, 128), F32),
-            pltpu.VMEM((NTM, 4, 8, 128), F32),
-            pltpu.VMEM((2, 4, 8, 128), F32),
-            pltpu.VMEM((NDP, 4, 8, 128), F32),
-            pltpu.VMEM((NTM, 4, 8, 128), F32),
+            pltpu.VMEM((NTM, 2, 16, 128), BF16),
+            pltpu.VMEM((2, 16, 128), BF16),
+            pltpu.VMEM((NDP, 2, 16, 128), BF16),
+            pltpu.VMEM((2, 16, 128), F32),
+            pltpu.VMEM((NTM, 2, 16, 128), F32),
             *rs_scratch((), 512),
             *rs_scratch((3,), 256),
             *rs_scratch((2,), 128),
@@ -746,8 +752,8 @@
             dma((NDP,)),
             dma((NTM,)),
             dma((NTM,)),
-            dma((NB, 10)),
-            dma((NB, 10)),
+            dma((NB, 19)),
+            dma((NB, 19)),
         ],
         compiler_params=pltpu.CompilerParams(
             collective_id=0, has_side_effects=True, vmem_limit_bytes=62 << 20

time: 90.4 us -> 91.7 us (1.014)
  no operation moved by 1% of the time
where the time goes in v4:
time: 91.7 us; the launch traced here: 90.9 us
  Pallas kernels  89.5 us (98%)
  between operations  1.45 us (2%)
    pallas_call x1, Pallas kernels, local(): pl.pallas_call(kernel, out_shape=(jax.ShapeDtypeStruct((ROWS, CH), BF16),...  86.5 us
    pallas_call x1, Pallas kernels, local(): pl.pallas_call(hand_over, out_shape=tuple((jax.ShapeDtypeStruct(o.shape,...  2.95 us

profile of v4, /device:TPU:0, one launch (start us, length us, event | category | flops | bytes accessed | tf_op | source)
XLA Modules:
  0.0 90.9 jit_solution(16917509473950226788)
XLA Ops:
  1.3 86.5 %conformer_conv.1 = (bf16[768,1024]{1,0:T(8,128)(2,1)}, bf16[768,1024]{1,0:T(8,128)(2,1)}, f32[8,2048]{1,0:T(8,128)}, f32[8,1024]{1,0:T(8,128)}, f32[31,1024]{1,...) custom-call(s32[1]{0:T(128)S(6)} %copy.15.len_ref, bf16[768,1024]{1,0:T(8,128)(2,1)} %bitcast.8, ...), custom_call_target="tpu_custom_call" | custom-call | tf_op jit(solution)/shard_map/conformer_conv/pallas_call | solution.py:693
  87.8 3.0 %hand_over.1 = (bf16[768,1024]{1,0:T(8,128)(2,1)}, bf16[768,1024]{1,0:T(8,128)(2,1)}, f32[8,2048]{1,0:T(8,128)}, f32[8,1024]{1,0:T(8,128)}, f32[31,1024]{1,0:T(8...) custom-call(bf16[768,1024]{1,0:T(8,128)(2,1)} %get-tuple-element.21.refs_0_, bf16[768,1024]{1,0:T(8,128)(2,1)} %get-tuple-element.22.refs_1_, ...), custom_call_target="tpu_custom_call" | custom-call | tf_op jit(solution)/shard_map/hand_over/pallas_call | solution.py:766

commit v5 on v4

--- a/solution.py
+++ b/solution.py
@@ -21,7 +21,7 @@
 NDP, NTM = 16, 8
 GRP = 12
 GROUPS = ROWS // (8 * GRP)
-NB = 6
+NB = 5
 ORDER = ("z", "x", "y")
 
 
@@ -49,8 +49,8 @@
     red, red_in, red_mid, red_rx1, red_rx2,
     gkl, gk1, gk2, gk3, kr1, ks1, kr2, ks2, kfull,
     wl_a, crx_a, cs_a, r1_a, s1_a, r2_a, s2_a, r3_a,
-    wl_b, crx_b, cs_b, r1_b, s1_b, r2_b, s2_b, r3_b,
-    wl_c, crx_c, cs_c, r1_c, s1_c, r2_c, s2_c, r3_c,
+    wl_b, crx_b, cs_b, r1_b, s1_b, r2_b,
+    wl_c, crx_c, cs_c, r1_c, s1_c, r2_c,
     in_sem, w_sem, out_sem, halo_s, halo_r, ar1_s, ar1_r, ar2_s, ar2_r,
     k1_s, k1_r, k2_s, k2_r, k3_s, k3_r, rs_s, rs_r,
 ):
@@ -184,23 +184,31 @@
     EDGE, INNER = 8, 16
 
     def conv_inner(cb):
-        s = sq = jnp.zeros((8, 128), F32)
-        for i in range((ROWS - 128) // 128):
-            s, sq = conv_rows(cb, 64 + i * 128, INNER, (s, sq))
+        def step(i, carry):
+            return conv_rows(cb, pl.multiple_of(64 + i * 128, 64), INNER, carry)
+
+        zero = jnp.zeros((8, 128), F32)
+        s, sq = lax.fori_loop(0, (ROWS - 128) // 128, step, (zero, zero))
         stat_v[cb, 0] = s
         stat_v[cb, 1] = sq
 
-    pl.loop(0, 2)(conv_inner)
-    pl.semaphore_wait(barrier, NTM + NDP - 2)
-    halo_g[0]()
-    pl.loop(2, CB)(conv_inner)
-    halo_g[1]()
+    def meet():
+        pl.semaphore_wait(barrier, NTM + NDP - 2)
+        halo_g[0]()
 
     @pl.loop(0, CB)
     def _(cb):
-        s, sq = stat_v[cb, 0], stat_v[cb, 1]
-        for row0 in (0, ROWS - 64):
-            s, sq = conv_rows(cb, row0, EDGE, (s, sq))
+        pl.when(cb == 2)(meet)
+        conv_inner(cb)
+
+    halo_g[1]()
+
+    @pl.loop(0, CB)
+    def _(cb):
+        def step(i, carry):
+            return conv_rows(cb, pl.multiple_of(i * (ROWS - 64), 64), EDGE, carry)
+
+        s, sq = lax.fori_loop(0, 2, step, (stat_v[cb, 0], stat_v[cb, 1]))
         red[0, pl.ds(cb, 1), :] = jnp.sum(s, axis=0, keepdims=True)
         red[1, pl.ds(cb, 1), :] = jnp.sum(sq, axis=0, keepdims=True)
 
@@ -362,15 +370,21 @@
 
     ar_b[0]()
 
+    A = ("a", None)
+    rs_bufs = {
+        "a": dict(wl=wl_a, crx=crx_a, cs=cs_a, r1=r1_a, s1=s1_a, r2=r2_a, s2=s2_a, r3=r3_a),
+        "y": dict(wl=wl_b, crx=crx_b, cs=cs_b, r1=r1_b, s1=s1_b, r2=r2_b),
+        "dp": dict(wl=wl_c, crx=crx_c, cs=cs_c, r1=r1_c, s1=s1_c, r2=r2_c),
+    }
+
     def buf(name, b):
-        whole, pairs, singles = rs_bufs[name]
-        return whole if b == 0 else pairs.at[b - 1] if b < 4 else singles.at[b - 4]
-
-    rs_bufs = {
-        "wl": (wl_a, wl_b, wl_c), "crx": (crx_a, crx_b, crx_c), "cs": (cs_a, cs_b, cs_c),
-        "r1": (r1_a, r1_b, r1_c), "s1": (s1_a, s1_b, s1_c), "r2": (r2_a, r2_b, r2_c),
-        "s2": (s2_a, s2_b, s2_c), "r3": (r3_a, r3_b, r3_c),
-    }
+        kind, i = b
+        ref = rs_bufs[kind][name]
+        return ref if kind == "a" else ref.at[i]
+
+    def number(b):
+        kind, i = b
+        return {"a": 0, "y": 1, "dp": 3}[kind] + (0 if kind == "a" else i)
 
     def put_terms(dst, rows, cols, first, second):
         n, w = first.shape[0] // 16, first.shape[1]
@@ -379,7 +393,8 @@
 
     def rs_core(b):
         return rcopy(
-            buf("wl", b).at[:, 1 - core], buf("crx", b), rs_s.at[b, 0], rs_r.at[b, 0],
+            buf("wl", b).at[:, 1 - core], buf("crx", b),
+            rs_s.at[number(b), 0], rs_r.at[number(b), 0],
             (dp, tm + 1 - 2 * core),
         )
 
@@ -388,15 +403,15 @@
         return ref.at[tuple(slice(None) for _ in range(at)) + (p,)]
 
     def rs_copies(b, stage):
-        dims = ("z", "x", "y")
-        if b == 0:
-            src, dst = (("cs", "r1"), ("s1", "r2"), ("s2", "r3"))[stage]
-            dims = tuple(a for a in dims if a not in ORDER[:stage])
-            axis = ORDER[stage]
+        src, dst = (("cs", "r1"), ("s1", "r2"), ("s2", "r3"))[stage]
+        src, dst = buf(src, b), buf(dst, b)
+        kind, n = b[0], number(b)
+        axis = {"a": ORDER, "y": ("y", "dp"), "dp": ("dp", "y")}[kind][stage]
+        if kind == "a":
+            dims = tuple(a for a in ("z", "x", "y") if a not in ORDER[:stage])
         else:
-            src, dst = (("cs", "r1"), ("s1", "r2"))[stage]
-            axis = ("y", "dp")[stage]
-        src, dst = buf(src, b), buf(dst, b)
+            dims = ("y",) if (kind, stage) == ("dp", 1) else ("z", "x", "y")
+        first_sem = {"a": 3, "y": 3, "dp": 15}[kind] * stage
         copies = []
         if axis == "dp":
             for d in range(1, NDP):
@@ -404,7 +419,7 @@
                 copies.append(
                     rcopy(
                         src.at[p // 4, p % 4], dst.at[d - 1],
-                        rs_s.at[b, 3 + d], rs_r.at[b, 3 + d], (p, tm),
+                        rs_s.at[n, first_sem + d], rs_r.at[n, first_sem + d], (p, tm),
                     )
                 )
             return copies, src.at[z, x], dst
@@ -413,13 +428,13 @@
             copies.append(
                 rcopy(
                     part_of(src, dims, axis, p), dst.at[d - 1],
-                    rs_s.at[b, 3 * stage + d], rs_r.at[b, 3 * stage + d], at_axis(axis, p),
+                    rs_s.at[n, first_sem + d], rs_r.at[n, first_sem + d], at_axis(axis, p),
                 )
             )
         return copies, part_of(src, dims, axis, pos[axis]), dst
 
     def stages(b):
-        return 3 if b == 0 else 2
+        return 3 if b == A else 2
 
     def rs_one(b):
         rs_core(b).wait_recv()
@@ -446,28 +461,28 @@
                 c.start()
         else:
             acc = acc * SCALE
-            if b == 0:
+            if b == A:
                 gwo_ref[:, 0:512] = acc[0:8]
                 gwo_ref[:, 512:1024] = acc[8:16]
             else:
-                c0, w = (256 * (b - 1), 256) if b < 4 else (128 * (b + 2), 128)
-                gwi_ref[:, c0 : c0 + w] = acc[0:8]
-                gwi_ref[:, CH + c0 : CH + c0 + w] = acc[8:16]
-
-    for half in range(2):
-        cols = slice(256 * half, 256 * half + 256)
-        for i in range(2):
-            rows = jnp.concatenate([sw_v[4 * i + e] for e in range(4)], axis=1)
-            put_terms(
-                wl_a, i, cols,
-                dot_tn(rows, cot[:, 256 * half : 256 * half + 256]),
-                dot_tn(rows, cot[:, 512 + 256 * half : 512 + 256 * half + 256]),
-            )
-
-    rs_core(0).start()
+                c0 = pl.multiple_of(512 * b[1] + (0 if b[0] == "y" else 256), 256)
+                gwi_ref[:, pl.ds(c0, 256)] = acc[0:8]
+                gwi_ref[:, pl.ds(CH + c0, 256)] = acc[8:16]
+
+    @pl.loop(0, 4)
+    def _(n):
+        half, i = n // 2, n % 2
+        c0 = pl.multiple_of(256 * half, 256)
+        rows = jnp.concatenate([sw_v[4 * i + e] for e in range(4)], axis=1)
+        put_terms(
+            wl_a, i, pl.ds(c0, 256),
+            dot_tn(rows, cot[:, pl.ds(c0, 256)]), dot_tn(rows, cot[:, pl.ds(512 + c0, 256)]),
+        )
+
+    rs_core(A).start()
     tap_sums(gk1, dsh_v, 2, ar_b[1])
     live_sums()
-    rs_one(0)
+    rs_one(A)
 
     grads = ar_b[2]()
     gg_ref[...] = grads[0] * SCALE
@@ -520,38 +535,14 @@
             dpre_v[cb, rows, :] = jnp.concatenate(dl, axis=0).astype(BF16)
             dpre_v[CB + cb, rows, :] = jnp.concatenate(dg, axis=0).astype(BF16)
 
-    def back_inner(cb):
-        for i in range((ROWS - 128) // 128):
-            back_rows(cb, 64 + 128 * i, INNER)
-
-    def back_edges(cb):
-        for row0 in (0, ROWS - 64):
-            back_rows(cb, row0, EDGE)
-
-    def back_all(cb):
-        for i in range(GROUPS):
-            back_rows(cb, 8 * GRP * i, GRP)
-
-    def pair_terms(j):
+    def pair_terms(j, b):
         first = jnp.concatenate([dpre_v[2 * j], dpre_v[2 * j + 1]], axis=1)
         second = jnp.concatenate([dpre_v[CB + 2 * j], dpre_v[CB + 2 * j + 1]], axis=1)
 
         @pl.loop(0, 2)
         def _(i):
             rows = feats[:, pl.ds(pl.multiple_of(512 * i, 512), 512)]
-            put_terms(buf("wl", 1 + j), i, slice(None), dot_tn(rows, first), dot_tn(rows, second))
-
-        rs_core(1 + j).start()
-
-    def single_terms(b):
-        cb = b + 2
-        both = jnp.concatenate([dpre_v[cb], dpre_v[CB + cb]], axis=1)
-
-        @pl.loop(0, 2)
-        def _(i):
-            rows = feats[:, pl.ds(pl.multiple_of(512 * i, 512), 512)]
-            part = dot_tn(rows, both)
-            put_terms(buf("wl", b), i, slice(None), part[:, 0:128], part[:, 128:256])
+            put_terms(buf("wl", b), i, slice(None), dot_tn(rows, first), dot_tn(rows, second))
 
         rs_core(b).start()
 
@@ -580,73 +571,84 @@
                     gk_ref[k : k + 1, 128 * cb : 128 * cb + 128] = row * SCALE
 
     def frame_cols(j):
+        c0 = pl.multiple_of(256 * j, 256)
         rows = jnp.concatenate([dpre_v[c] for c in range(2 * CB)], axis=1)
-        part = dot_nt(rows, w_in[256 * j : 256 * j + 256, :])
-        out_v[1, :, 256 * j : 256 * j + 256] = part.astype(BF16)
+        out_v[1, :, pl.ds(c0, 256)] = dot_nt(rows, w_in[pl.ds(c0, 256), :]).astype(BF16)
 
     def out_cols(j):
+        c0 = pl.multiple_of(256 * j, 256)
         rows = jnp.concatenate([sw_v[cb] for cb in range(CB)], axis=1)
-        part = dot_nn(rows, w_out[:, 256 * j : 256 * j + 256])
-        out_v[0, :, 256 * j : 256 * j + 256] = part.astype(BF16)
+        out_v[0, :, pl.ds(c0, 256)] = dot_nn(rows, w_out[:, pl.ds(c0, 256)]).astype(BF16)
 
     kt_sum(0)
     dconv_rows(((PAD, 384), (PAD + 384, 352)))
-    pl.loop(0, 2)(back_inner)
-    halo_d[1]()
-    pl.loop(0, 2)(back_edges)
-    pair_terms(0)
-    kt_sum(1)
-    pl.loop(2, 4)(back_all)
-    pair_terms(1)
-    rs_one(1)
-    pl.loop(4, 6)(back_all)
-    pair_terms(2)
-    rs_one(2)
-    kt_sum(2)
-    rs_next(0, 0)
-    pl.loop(6, 7)(back_all)
-    single_terms(4)
-    rs_one(3)
-    pl.loop(7, 8)(back_all)
-    single_terms(5)
-    rs_one(4)
-
-    frame_cols(0)
-    rs_one(5)
-    rs_next(1, 0)
-    frame_cols(1)
-    frame_cols(2)
-    rs_next(0, 1)
-    frame_cols(3)
+
+    def back_pair(j, at_row):
+        @pl.loop(0, 6)
+        def _(i):
+            at_row(i)
+            row0 = pl.multiple_of((i + 1) % 6 * 128, 128)
+
+            @pl.loop(0, 2)
+            def _(h):
+                back_rows(2 * j + h, row0, 16)
+
+    @pl.loop(0, 2)
+    def _(n):
+        def even(i):
+            pl.when((n == 0) & (i == 4))(halo_d[1])
+            pl.when((n == 1) & (i == 5))(lambda: rs_one(("dp", 0)))
+
+        def odd(i):
+            pl.when(i == 5)(lambda: rs_one(("y", n)))
+
+        back_pair(2 * n, even)
+        pair_terms(2 * n, ("y", n))
+        pl.when(n == 0)(lambda: kt_sum(1))
+        back_pair(2 * n + 1, odd)
+        pair_terms(2 * n + 1, ("dp", n))
+        pl.when(n == 0)(lambda: kt_sum(2))
+        pl.when(n == 1)(lambda: rs_next(A, 0))
+
+    @pl.loop(0, 8)
+    def _(n):
+        pl.when(n < 4)(lambda: frame_cols(n))
+        pl.when(n >= 4)(lambda: out_cols(n - 4))
+        pl.when(n == 0)(lambda: rs_one(("dp", 1)))
+        pl.when(n == 4)(lambda: rs_next(A, 1))
+        pl.when((n == 3) | (n == 7))(lambda: rs_next(("y", n // 4), 0))
+        pl.when(n == 5)(lambda: rs_next(("dp", 0), 0))
+
     gf_copy = pltpu.make_async_copy(out_v.at[1], gf_h, out_sem.at[1])
     gf_copy.start()
-    rs_next(2, 0)
-    out_cols(0)
-    out_cols(1)
-    rs_next(3, 0)
-    out_cols(2)
-    out_cols(3)
     out_copy = pltpu.make_async_copy(out_v.at[0], out_h, out_sem.at[0])
     out_copy.start()
-    rs_next(4, 0)
-    rs_next(5, 0)
+    rs_next(("dp", 1), 0)
     kt_sum(3)
-    rs_next(0, 2)
-    rs_next(1, 1)
-    rs_next(2, 1)
-    rs_next(3, 1)
-    rs_next(4, 1)
-    rs_next(5, 1)
+    rs_next(A, 2)
+
+    @pl.loop(0, 2)
+    def _(n):
+        rs_next(("y", n), 1)
+        rs_next(("dp", n), 1)
 
     for t in (halo_g, halo_d, kt1, kt2, kt3):
         t[2]()
     ar_a[3]()
     ar_b[3]()
-    for b in range(NB):
+    def block_sent(b):
         rs_core(b).wait_send()
         for stage in range(stages(b)):
             for c in rs_copies(b, stage)[0]:
                 c.wait_send()
+
+    block_sent(A)
+
+    @pl.loop(0, 2)
+    def _(n):
+        block_sent(("y", n))
+        block_sent(("dp", n))
+
     out_copy.wait()
     gf_copy.wait()
 
@@ -654,10 +656,14 @@
 SCALE = 1.0 / math.sqrt(16 * 6144)
 
 
-def rs_scratch(lead, width):
-    shapes = [(64, 2), (64,), (4, 4, 4), (3, 4, 4), (4, 4), (3, 4), (4,), (3,)]
-    if lead:
-        shapes[5:] = [(15,), (1,), (1,)]
+def rs_scratch(kind):
+    shapes = [(64, 2), (64,), (4, 4, 4)]
+    shapes += {
+        "a": [(3, 4, 4), (4, 4), (3, 4), (4,), (3,)],
+        "y": [(3, 4, 4), (4, 4), (15,)],
+        "dp": [(15, 4), (4,), (3,)],
+    }[kind]
+    lead, width = ((), 512) if kind == "a" else ((2,), 256)
     return [pltpu.VMEM((*lead, *s, 16, width), BF16) for s in shapes]
 
 
@@ -734,9 +740,9 @@
             pltpu.VMEM((NDP, 2, 16, 128), BF16),
             pltpu.VMEM((2, 16, 128), F32),
             pltpu.VMEM((NTM, 2, 16, 128), F32),
-            *rs_scratch((), 512),
-            *rs_scratch((3,), 256),
-            *rs_scratch((2,), 128),
+            *rs_scratch("a"),
+            *rs_scratch("y"),
+            *rs_scratch("dp"),
             dma((3,)),
             dma((4, 2)),
             dma((2,)),

time: 91.7 us -> 90 us (0.981)
  no operation moved by 1% of the time
where the time goes in v5:
time: 90 us; the launch traced here: 89.9 us
  Pallas kernels  88.6 us (98%)
  between operations  1.29 us (1%)
    pallas_call x1, Pallas kernels, local(): pl.pallas_call(kernel, out_shape=(jax.ShapeDtypeStruct((ROWS, CH), BF16),...  85.6 us
    pallas_call x1, Pallas kernels, local(): pl.pallas_call(hand_over, out_shape=tuple((jax.ShapeDtypeStruct(o.shape,...  2.95 us

profile of v5, /device:TPU:0, one launch (start us, length us, event | category | flops | bytes accessed | tf_op | source)
XLA Modules:
  0.0 89.9 jit_solution(17809108361468121501)
XLA Ops:
  1.3 85.6 %conformer_conv.1 = (bf16[768,1024]{1,0:T(8,128)(2,1)}, bf16[768,1024]{1,0:T(8,128)(2,1)}, f32[8,2048]{1,0:T(8,128)}, f32[8,1024]{1,0:T(8,128)}, f32[31,1024]{1,...) custom-call(s32[1]{0:T(128)S(6)} %copy.15.len_ref, bf16[768,1024]{1,0:T(8,128)(2,1)} %bitcast.8, ...), custom_call_target="tpu_custom_call" | custom-call | tf_op jit(solution)/shard_map/conformer_conv/pallas_call | solution.py:699
  86.9 3.0 %hand_over.1 = (bf16[768,1024]{1,0:T(8,128)(2,1)}, bf16[768,1024]{1,0:T(8,128)(2,1)}, f32[8,2048]{1,0:T(8,128)}, f32[8,1024]{1,0:T(8,128)}, f32[31,1024]{1,0:T(8...) custom-call(bf16[768,1024]{1,0:T(8,128)(2,1)} %get-tuple-element.21.refs_0_, bf16[768,1024]{1,0:T(8,128)(2,1)} %get-tuple-element.22.refs_1_, ...), custom_call_target="tpu_custom_call" | custom-call | tf_op jit(solution)/shard_map/hand_over/pallas_call | solution.py:772

commit v6 on v5

--- a/solution.py
+++ b/solution.py
@@ -280,12 +280,13 @@
         for h in range(2):
             dsh_v[2 * j + h] = ds[:, h * 128 : h * 128 + 128]
 
-    def tap_sums(dst, grad, first_blocks, between):
+    def tap_sums(dst, grad, *between):
         grp = 16
 
         @pl.loop(0, CB)
         def _(cb):
-            pl.when(cb == first_blocks)(between)
+            for blocks, call in between:
+                pl.when(cb == blocks)(call)
 
             def step(i, accs):
                 row0 = pl.multiple_of(i * (8 * grp), 8 * grp)
@@ -327,7 +328,7 @@
                 outer, ends.astype(BF16)
             )
 
-    tap_sums(gk3, conv_v, 1, ar_a[1])
+    tap_sums(gk3, conv_v, (1, ar_a[1]))
     sums = ar_a[2]()
     mean = sums[0] * (1.0 / COUNT)
     variance = sums[1] * (1.0 / COUNT) - mean * mean
@@ -480,9 +481,8 @@
         )
 
     rs_core(A).start()
-    tap_sums(gk1, dsh_v, 2, ar_b[1])
+    tap_sums(gk1, dsh_v, (2, ar_b[1]), (5, lambda: rs_one(A)))
     live_sums()
-    rs_one(A)
 
     grads = ar_b[2]()
     gg_ref[...] = grads[0] * SCALE
@@ -608,14 +608,15 @@
         back_pair(2 * n + 1, odd)
         pair_terms(2 * n + 1, ("dp", n))
         pl.when(n == 0)(lambda: kt_sum(2))
-        pl.when(n == 1)(lambda: rs_next(A, 0))
+        pl.when(n == 0)(lambda: rs_next(A, 0))
+        pl.when(n == 1)(lambda: rs_next(A, 1))
 
     @pl.loop(0, 8)
     def _(n):
         pl.when(n < 4)(lambda: frame_cols(n))
         pl.when(n >= 4)(lambda: out_cols(n - 4))
         pl.when(n == 0)(lambda: rs_one(("dp", 1)))
-        pl.when(n == 4)(lambda: rs_next(A, 1))
+        pl.when(n == 4)(lambda: rs_next(A, 2))
         pl.when((n == 3) | (n == 7))(lambda: rs_next(("y", n // 4), 0))
         pl.when(n == 5)(lambda: rs_next(("dp", 0), 0))
 
@@ -625,7 +626,6 @@
     out_copy.start()
     rs_next(("dp", 1), 0)
     kt_sum(3)
-    rs_next(A, 2)
 
     @pl.loop(0, 2)
     def _(n):

time: 90 us -> 86.1 us (0.957)
  Pallas kernels: 88.6 us -> 84.6 us
    pallas_call x1, Pallas kernels: 85.6 us -> 81.7 us  [local(): pl.pallas_call(kernel, out_shape=(jax.ShapeDtypeStruct((ROWS, CH), BF16),...]
where the time goes in v6:
time: 86.1 us; the launch traced here: 85.9 us
  Pallas kernels  84.6 us (98%)
  between operations  1.29 us (1%)
    pallas_call x1, Pallas kernels, local(): pl.pallas_call(kernel, out_shape=(jax.ShapeDtypeStruct((ROWS, CH), BF16),...  81.7 us
    pallas_call x1, Pallas kernels, local(): pl.pallas_call(hand_over, out_shape=tuple((jax.ShapeDtypeStruct(o.shape,...  2.95 us

profile of v6, /device:TPU:0, one launch (start us, length us, event | category | flops | bytes accessed | tf_op | source)
XLA Modules:
  0.0 85.9 jit_solution(14017920358732331031)
XLA Ops:
  1.3 81.7 %conformer_conv.1 = (bf16[768,1024]{1,0:T(8,128)(2,1)}, bf16[768,1024]{1,0:T(8,128)(2,1)}, f32[8,2048]{1,0:T(8,128)}, f32[8,1024]{1,0:T(8,128)}, f32[31,1024]{1,...) custom-call(s32[1]{0:T(128)S(6)} %copy.15.len_ref, bf16[768,1024]{1,0:T(8,128)(2,1)} %bitcast.8, ...), custom_call_target="tpu_custom_call" | custom-call | tf_op jit(solution)/shard_map/conformer_conv/pallas_call | solution.py:699
  82.9 3.0 %hand_over.1 = (bf16[768,1024]{1,0:T(8,128)(2,1)}, bf16[768,1024]{1,0:T(8,128)(2,1)}, f32[8,2048]{1,0:T(8,128)}, f32[8,1024]{1,0:T(8,128)}, f32[31,1024]{1,0:T(8...) custom-call(bf16[768,1024]{1,0:T(8,128)(2,1)} %get-tuple-element.21.refs_0_, bf16[768,1024]{1,0:T(8,128)(2,1)} %get-tuple-element.22.refs_1_, ...), custom_call_target="tpu_custom_call" | custom-call | tf_op jit(solution)/shard_map/hand_over/pallas_call | solution.py:772
